TPU v7x, 128 devices: a whole 4x4x4 slice. The times are simulated.
128 devices in a mesh: frame: 16 (over z, x_lo, core), patch: 8 (over x_hi, y).
Axes of the slice: x: 4 (x_hi: 2, x_lo: 2; x = x_hi * 2 + x_lo), y: 4, z: 4, core: 2. Of those that a mesh axis runs over, the one named last changes fastest.
Arguments:
- coeffs: float32 [32, 128, 300], P('frame', 'patch'), may hold values from -4 to 4
- observed: bfloat16 [32, 128, 128, 128], P('frame', 'patch'), may hold values from -6 to 6
- object_field: float32 [128, 128, 128], P('patch', 'frame'), may hold values from -6 to 6
- mode_basis: bfloat16 [300, 128, 128], replicated, may hold values from -0.375 to 0.375
- pupil_mask: int32 [128, 128], replicated, may hold values from 0 to 1, as said below
Outputs:
- new_coeffs: float32 [32, 128, 300], P('frame', 'patch')
- new_object: float32 [128, 128, 128], P('patch', 'frame')
Inputs may be any that keep to these rules, and one draw needn't show every extreme that they name: `pupil_mask`: the pupil is an annulus centred on cell 128 // 2 of each dimension with an outer radius of at least 48 cells, so it holds ones.
All inputs are finite; a program needn't handle non-finite values.
Results may differ from a plain program's by a relative error of at most 0.0035.
Values may be sent and summed in bfloat16 or wider, within the bound.
A program may use at most 128 MiB of HBM per device.

v0:
```python
import math

import jax
import jax.numpy as jnp
from jax import lax
from jax.sharding import PartitionSpec as P

ITERS = 2


EPSILON = 1e-06
STEP_OBJECT = 0.1
STEP_COEFF = 0.2


def dft_tables(extent):
    counter = jnp.arange(extent, dtype=jnp.int32)
    product = counter[:, None] * counter[None, :] % extent
    angles = product.astype(jnp.float32) * (2.0 * math.pi / extent)
    return (jnp.cos(angles).astype(jnp.bfloat16), jnp.sin(angles).astype(jnp.bfloat16))


def right_mul(values, matrix):
    in_shape = values.shape
    result = jnp.dot(values.reshape(-1, in_shape[-1]), matrix, preferred_element_type=jnp.float32)
    return result.reshape(in_shape)


def left_mul(values, matrix):
    return jnp.einsum("jb,nbk->njk", matrix, values, preferred_element_type=jnp.float32)


def apply_pass(multiply, real_in, imag_in, cosine, sine_table, inverse, keep_imag):
    sign_value = 1.0 if inverse else -1.0
    real_low = real_in.astype(jnp.bfloat16)
    out_real = multiply(real_low, cosine)
    if imag_in is not None:
        imag_low = imag_in.astype(jnp.bfloat16)
        out_real = out_real - sign_value * multiply(imag_low, sine_table)
    if not keep_imag:
        return (out_real, None)
    out_imag = sign_value * multiply(real_low, sine_table)
    if imag_in is not None:
        out_imag = out_imag + multiply(imag_low, cosine)
    return (out_real, out_imag)


def transform(real_in, imag_in, cosine, sine_table, inverse, keep_imag):
    first_real, first_imag = apply_pass(
        right_mul, real_in, imag_in, cosine, sine_table, inverse, True
    )
    return apply_pass(left_mul, first_real, first_imag, cosine, sine_table, inverse, keep_imag)


def pair_terms(
    coeff_rows,
    observed_rows,
    spec_real,
    spec_imag,
    flat_basis,
    aperture,
    psf_scale,
    cosine,
    sine_table,
):
    pairs = coeff_rows.shape[0]
    extent = observed_rows.shape[-1]
    phase_map = jnp.dot(
        coeff_rows.astype(jnp.bfloat16), flat_basis, preferred_element_type=jnp.float32
    ).reshape(pairs, extent, extent)
    cos_phase = jnp.cos(phase_map)
    sin_phase = jnp.sin(phase_map)
    focal_real, focal_imag = transform(
        aperture * cos_phase, aperture * sin_phase, cosine, sine_table, False, True
    )
    spread = (focal_real * focal_real + focal_imag * focal_imag) * psf_scale
    otf_real, otf_imag = transform(spread, None, cosine, sine_table, False, True)
    model_real = spec_real * otf_real - spec_imag * otf_imag
    model_imag = spec_real * otf_imag + spec_imag * otf_real
    model_image, unused = transform(model_real, model_imag, cosine, sine_table, True, False)
    residual = model_image / (extent * extent) - observed_rows.astype(jnp.float32)
    grad_real, grad_imag = transform(residual, None, cosine, sine_table, False, True)
    grad_real = grad_real / (extent * extent)
    grad_imag = grad_imag / (extent * extent)
    objg_real = grad_real * otf_real + grad_imag * otf_imag
    objg_imag = grad_imag * otf_real - grad_real * otf_imag
    half_real, half_imag = apply_pass(
        right_mul, objg_real, objg_imag, cosine, sine_table, True, True
    )
    otfg_real = grad_real * spec_real + grad_imag * spec_imag
    otfg_imag = grad_imag * spec_real - grad_real * spec_imag
    spread_grad, unused = transform(otfg_real, otfg_imag, cosine, sine_table, True, False)
    factor = 2.0 * psf_scale * spread_grad
    field_real, field_imag = transform(
        factor * focal_real, factor * focal_imag, cosine, sine_table, True, True
    )
    phase_grad = aperture * (field_imag * cos_phase - field_real * sin_phase)
    coeff_grad = lax.dot_general(
        phase_grad.reshape(pairs, -1).astype(jnp.bfloat16),
        flat_basis,
        (((1,), (1,)), ((), ())),
        preferred_element_type=jnp.float32,
    )
    return (coeff_grad, half_real, half_imag)


def shards(coeffs, observed, object_field, mode_basis, pupil_mask):
    frames_dev, patches_dev, mode_count = coeffs.shape
    extent = mode_basis.shape[-1]
    rows_dev = object_field.shape[1]
    pairs = frames_dev * patches_dev
    cosine, sine_table = dft_tables(extent)
    aperture = pupil_mask.astype(jnp.float32)
    psf_scale = 1.0 / (extent * extent * jnp.sum(aperture))
    flat_basis = mode_basis.reshape(mode_count, extent * extent)
    observed_rows = observed.reshape(pairs, extent, extent)
    row_start = lax.axis_index("frame") * rows_dev
    object_total = object_field.size * lax.axis_size("frame") * lax.axis_size("patch")
    coeff_total = coeffs.size * lax.axis_size("frame") * lax.axis_size("patch")
    empty = jnp.zeros((patches_dev, extent, extent), jnp.float32)
    for iteration in range(ITERS):
        piece_rows = lax.all_gather(object_field.astype(jnp.bfloat16), "frame", axis=1, tiled=True)
        add_real = jnp.einsum("jb,nbk->njk", cosine, piece_rows, preferred_element_type=jnp.float32)
        add_imag = jnp.einsum(
            "jb,nbk->njk", sine_table, piece_rows, preferred_element_type=jnp.float32
        )
        rows_imag = (empty, empty)[1] - add_imag
        spec_real, spec_imag = apply_pass(
            right_mul, add_real, rows_imag, cosine, sine_table, False, True
        )
        spec_real = jnp.broadcast_to(
            spec_real[None], (frames_dev, patches_dev, extent, extent)
        ).reshape(pairs, extent, extent)
        spec_imag = jnp.broadcast_to(
            spec_imag[None], (frames_dev, patches_dev, extent, extent)
        ).reshape(pairs, extent, extent)
        coeff_grad, half_real, half_imag = pair_terms(
            coeffs.reshape(pairs, mode_count),
            observed_rows,
            spec_real,
            spec_imag,
            flat_basis,
            aperture,
            psf_scale,
            cosine,
            sine_table,
        )
        half_real = half_real.astype(jnp.bfloat16).reshape(frames_dev, patches_dev, extent, extent)
        half_imag = half_imag.astype(jnp.bfloat16).reshape(frames_dev, patches_dev, extent, extent)
        full_real = jnp.einsum(
            "jb,fnbk->njk", cosine, half_real, preferred_element_type=jnp.float32
        )
        full_imag = jnp.einsum(
            "jb,fnbk->njk", sine_table, half_imag, preferred_element_type=jnp.float32
        )
        summed = lax.psum((full_real - full_imag).astype(jnp.bfloat16), "frame").astype(jnp.float32)
        own_grad = lax.dynamic_slice_in_dim(summed, row_start, rows_dev, 1)
        object_sq, coeff_sq = lax.psum(
            (jnp.sum(own_grad * own_grad), jnp.sum(coeff_grad * coeff_grad)), ("frame", "patch")
        )
        object_rms = jnp.sqrt(object_sq / object_total + EPSILON)
        coeff_rms = jnp.sqrt(coeff_sq / coeff_total + EPSILON)
        object_field = object_field - STEP_OBJECT * own_grad / object_rms
        coeffs = coeffs - STEP_COEFF * coeff_grad.reshape(coeffs.shape) / coeff_rms
    return (coeffs, object_field)


def solution(mesh):
    in_specs = (
        P("frame", "patch", None),
        P("frame", "patch", None, None),
        P("patch", "frame", None),
        P(),
        P(),
    )
    out_specs = (P("frame", "patch", None), P("patch", "frame", None))
    return jax.shard_map(shards, mesh=mesh, in_specs=in_specs, out_specs=out_specs, check_vma=False)
```

profile of v0, /device:TPU:1, one launch (start us, length us, event | category | flops | bytes accessed | tf_op | source)
XLA Modules:
  0.0 617.9 jit_solution(4033103090098036555)
XLA Ops:
  7.2 12.0 %slice_bitcast_fusion = bf16[128,128,300]{1,0,2:T(8,128)(2,1)} fusion(bf16[300,128,128]{2,1,0:T(8,128)(2,1)} %param.8), kind=kLoop, calls=%fused_computation | loop fusion | bytes 19660800 | tf_op jit(solution)/shard_map/dot_general | solution.py:68
  19.3 12.7 %fusion.671 = (f32[32,128,128]{2,0,1:T(8,128)S(1)}, f32[32,128,128]{2,0,1:T(8,128)S(1)}) fusion(bf16[32,300,1]{1,0,2:T(8,128)(2,1)S(1)} %bitcast.461, bf16[128,128,300]{1,0,2:T(8,128)(2,1)} %slice_bitcast_fusion), kind=kOutput, calls=%fused_computation.634 | convolution fusion | flops 314572800 | bytes 14043904 | tf_op jit(solution)/shard_map/dot_general | solution.py:68
  50.1 24.7 %all_gather.6 = bf16[16,128,128]{2,1,0:T(8,128)(2,1)S(1)} all-gather(bf16[16,8,128]{2,1,0:T(8,128)(2,1)S(1)} %convert_element_type.692), channel_id=1, replica_groups=mesh['frame'=16,'patch'=8] {'frame'}, dimensions={1}, use_global_device_ids=true | all-gather | bytes 557056 | tf_op jit(solution)/shard_map/all_gather | solution.py:122
  78.4 2.6 copy.269
  87.9 2.8 fusion.11
  94.7 3.0 copy.292
  97.7 4.1 fusion.40
  101.8 4.3 fusion.39
  111.1 2.8 fusion.38
  123.1 4.2 fusion.41
  127.4 5.4 fusion.63
  142.8 3.3 copy.312
  148.2 3.1 copy.311
  151.3 3.2 copy.315
  154.5 13.5 %multiply_reduce_fusion.1 = (f32[]{:T(128)}, f32[32,300]{1,0:T(8,128)S(1)}) fusion(bf16[300,128,128]{2,1,0:T(8,128)(2,1)} %param.8, f32[32,128,128]{2,0,1:T(8,128)} %copy-done.7, f32[32,128,128]{2,0,1:T(8,128)S(1)} %copy-done.6, f32[32,128,128]{1,0,2:T(8,128)} %copy.315, f32[32,128,128]{1,0,2:T(8,128)} %copy.316, f32[32,128,128]{1,0,2:T(8,128)} %copy.311, ...), kind=kOutput, calls=%fused_computation.202 | convolution fusion | flops 318262016 | bytes 22517252 | tf_op jit(solution)/shard_map/dot_general | solution.py:98
  168.0 67.9 %all-reduce.5.cloned.1.call-done = bf16[16,128,128]{2,1,0:T(8,128)(2,1)} async-done(((bf16[16,128,128]{2,1,0:T(8,128)(2,1)}), bf16[16,128,128]{2,1,0:T(8,128)(2,1)}) %all-reduce.5.cloned.1.call-update) | async-done | bytes 524304 | tf_op jit(solution)/shard_map/psum | solution.py:156
  237.3 67.0 %all-reduce.1 = (f32[]{:T(128)}, f32[]{:T(128)}) all-reduce(f32[]{:T(128)} %get-tuple-element.44, f32[]{:T(128)} %fusion.86), channel_id=1, replica_groups=mesh['frame'=16,'patch'=8] {'frame','patch'}, use_global_device_ids=true, to_apply=%region_2.3 | all-reduce | flops 2 | bytes 16 | tf_op jit(solution)/shard_map/psum | solution.py:158
  305.8 20.4 %all_gather.7 = bf16[16,128,128]{2,0,1:T(8,128)(2,1)S(1)} all-gather(bf16[16,8,128]{2,0,1:T(8,128)(2,1)S(1)} %copy.326), channel_id=1, replica_groups=mesh['frame'=16,'patch'=8] {'frame'}, dimensions={1}, use_global_device_ids=true | all-gather | bytes 557056 | tf_op jit(solution)/shard_map/all_gather | solution.py:122
  330.0 13.0 %fusion.670 = (f32[32,128,128]{2,0,1:T(8,128)S(1)}, f32[32,128,128]{2,0,1:T(8,128)S(1)}) fusion(bf16[32,300,1]{1,0,2:T(8,128)(2,1)S(1)} %bitcast.462, bf16[128,128,300]{1,0,2:T(8,128)(2,1)} %slice_bitcast_fusion), kind=kOutput, calls=%fused_computation.633 | convolution fusion | flops 314572800 | bytes 14043904 | tf_op jit(solution)/shard_map/dot_general | solution.py:68
  360.0 2.6 copy.331
  368.4 3.0 fusion.19
  375.4 4.1 fusion.42
  379.5 4.3 fusion.31
  388.8 2.8 fusion.30
  399.7 4.5 fusion.43
  404.2 5.3 fusion.65
  424.4 3.1 copy.375
  429.5 3.1 copy.374
  432.5 3.5 copy.378
  436.1 13.5 %multiply_reduce_fusion = (f32[]{:T(128)}, f32[32,300]{1,0:T(8,128)S(1)}) fusion(bf16[300,128,128]{2,1,0:T(8,128)(2,1)} %param.8, f32[32,128,128]{2,0,1:T(8,128)} %copy-done.10, f32[32,128,128]{2,0,1:T(8,128)S(1)} %copy-done.9, f32[32,128,128]{1,0,2:T(8,128)} %copy.378, f32[32,128,128]{1,0,2:T(8,128)} %copy.379, f32[32,128,128]{1,0,2:T(8,128)} %copy.374, ...), kind=kOutput, calls=%fused_computation.200 | convolution fusion | flops 318262016 | bytes 22517252 | tf_op jit(solution)/shard_map/dot_general | solution.py:98
  449.6 89.3 %all-reduce.7.cloned.1.call-done = bf16[16,128,128]{2,1,0:T(8,128)(2,1)} async-done(((bf16[16,128,128]{2,1,0:T(8,128)(2,1)}), bf16[16,128,128]{2,1,0:T(8,128)(2,1)}) %all-reduce.7.cloned.1.call-update) | async-done | bytes 524304 | tf_op jit(solution)/shard_map/psum | solution.py:156
  540.3 67.0 %all-reduce = (f32[]{:T(128)}, f32[]{:T(128)}) all-reduce(f32[]{:T(128)} %get-tuple-element.48, f32[]{:T(128)} %fusion.89), channel_id=1, replica_groups=mesh['frame'=16,'patch'=8] {'frame','patch'}, use_global_device_ids=true, to_apply=%region_9.10 | all-reduce | flops 2 | bytes 16 | tf_op jit(solution)/shard_map/psum | solution.py:158
  (187 shorter events, 123.2 us)
Async XLA Ops:
  7.2 12.1 %copy-start.36 = (f32[2,16,300]{2,1,0:T(8,128)S(1)}, f32[2,16,300]{2,1,0:T(8,128)}, u32[]{:S(2)}) copy-start(f32[2,16,300]{2,1,0:T(8,128)} %param.5) | copy-start | bytes 115204
  7.2 12.1 %copy-start.35 = (s32[128,128]{1,0:T(8,128)S(1)}, s32[128,128]{1,0:T(8,128)}, u32[]{:S(2)}) copy-start(s32[128,128]{1,0:T(8,128)} %param.9) | copy-start | bytes 196612
  7.2 228.7 %all-reduce.5.cloned.1.call-start = ((), (), s32[]{:S(2)}) async-start(), calls=%async_computation | async-start | bytes 1048576 | tf_op jit(solution)/shard_map/psum | solution.py:156
  32.0 2.0 copy-start.7
  39.9 2.7 copy-start
  48.0 2.0 copy-start.34
  85.0 2.4 copy-start.19
  85.0 2.4 copy-start.23
  85.0 2.9 copy-start.31
  94.7 3.0 copy-start.16
  108.9 1.5 copy-start.24
  108.9 2.2 copy-start.29
  113.9 9.3 %copy-start.13 = (bf16[32,128,128]{1,2,0:T(8,128)(2,1)}, bf16[32,128,128]{1,2,0:T(8,128)(2,1)S(1)}, u32[]{:S(2)}) copy-start(bf16[32,128,128]{1,2,0:T(8,128)(2,1)S(1)} %get-tuple-element.29) | copy-start | bytes 3145732
  117.0 2.1 copy-start.14
  118.8 420.1 %all-reduce.7.cloned.1.call-start = ((), (), s32[]{:S(2)}) async-start(), calls=%async_computation.1 | async-start | bytes 1048576 | tf_op jit(solution)/shard_map/psum | solution.py:156
  123.1 4.2 copy-start.1
  151.3 3.3 copy-start.6
  343.0 2.0 copy-start.10
  350.3 1.4 copy-start.2
  356.4 2.0 copy-start.33
  365.5 2.4 copy-start.21
  365.5 2.4 copy-start.25
  365.5 2.9 copy-start.32
  373.4 2.0 copy-start.17
  386.6 1.5 copy-start.26
  386.6 2.2 copy-start.30
  391.6 8.1 %copy-start.15 = (bf16[32,128,128]{1,2,0:T(8,128)(2,1)}, bf16[32,128,128]{1,2,0:T(8,128)(2,1)S(1)}, u32[]{:S(2)}) copy-start(bf16[32,128,128]{1,2,0:T(8,128)(2,1)S(1)} %get-tuple-element.27) | copy-start | bytes 3145732
  399.7 4.5 copy-start.3
  417.6 2.0 copy-start.18
  417.6 2.5 copy-start.28
  420.1 1.6 copy-start.27
  432.5 3.5 copy-start.9
  (7 other events, 8.9 us)
Sparse Core Ops, SparseCore 0:
  119.0 116.9 all-reduce.4
  424.6 114.3 all-reduce.6
where the time goes:
time: 622 us; the launch traced here: 618 us
  matrix products  194 us (31%)
  blocking collectives  179 us (29%)
  waiting for transfers between devices  157 us (25%)
  local copies, waits for them, and re-layouts  57.8 us (9%)
  between operations  18.5 us (3%)
  other arithmetic  10.7 us (2%)
    psum x2, waiting for transfers between devices, shards(): lax.psum((full_real - full_imag).astype(jnp.bfloat16), 'frame')  157 us
    psum x2, blocking collectives, shards(): lax.psum((jnp.sum(own_grad * own_grad), jnp.sum(coeff_grad * coeff_grad))...  134 us
    dot_general x40, matrix products, left_mul(): jnp.einsum('jb,nbk->njk', matrix, values, preferred_element_type=jnp.floa...  85 us
    dot_general x48, matrix products, right_mul(): jnp.dot(values.reshape(-1, in_shape[-1]), matrix, preferred_element_type=...  49.9 us
    all_gather x2, blocking collectives, shards(): lax.all_gather(object_field.astype(jnp.bfloat16), 'frame', axis=1, tiled=...  45.1 us
    dot_general x2, matrix products, pair_terms(): lax.dot_general(phase_grad.reshape(pairs, -1).astype(jnp.bfloat16), flat_...  27 us
    dot_general x2, matrix products, pair_terms(): jnp.dot(coeff_rows.astype(jnp.bfloat16), flat_basis, preferred_element_ty...  25.8 us
    dot_general x8, local copies, waits for them, and re-layouts, left_mul(): jnp.einsum('jb,nbk->njk', matrix, values, preferred_element_type=jnp.floa...  23.4 us
  transfers between devices with their start and end apart: 2, of which 2 were waited for; matrix products, arithmetic and copies ran while one was open for 12% of the time, Pallas kernels for 0%

commit v1 on v0

v1 whole, which is shorter than its diff:
```python
import functools
import math

import jax
import jax.numpy as jnp
import numpy as np
from jax import lax
from jax.experimental import pallas as pl
from jax.experimental.pallas import tpu as pltpu
from jax.sharding import PartitionSpec as P

ITERS = 2
EPSILON = 1e-06
STEP_OBJECT = 0.1
STEP_COEFF = 0.2
CHUNK = 8
BLK = 16
LANES = 128
MESH = pl.DeviceIdType.MESH
BF = jnp.bfloat16
F32 = jnp.float32


def fit(even):
    f = np.cos((np.arange(4000) + 0.5) * (np.pi / 8000)) * 0.5
    target = np.sqrt(2.0) * (np.cos(np.pi * f) if even else np.sin(np.pi * f) / f)
    powers = np.stack([f ** (2 * k) for k in range(6 if even else 5)], axis=1)
    coef = np.linalg.lstsq(powers, target, rcond=None)[0]
    return [float(np.float32(v)) for v in coef]


SIN_COEF = fit(False)
COS_COEF = fit(True)


def horner(z, coef):
    acc = coef[-1] * z + coef[-2]
    for value in coef[-3::-1]:
        acc = acc * z + value
    return acc


def sincos(x):
    turns = x * (1.0 / (2.0 * math.pi))
    f = turns - jnp.round(turns)
    z = f * f
    s = f * horner(z, SIN_COEF)
    c = horner(z, COS_COEF)
    return s * c, 1.0 - s * s


def dot(a, b):
    return jnp.dot(a, b, preferred_element_type=F32)


def swap_blocks(m):
    n = LANES
    return jnp.concatenate(
        [
            jnp.concatenate([m[:n, :n], m[n:, :n]], axis=1),
            jnp.concatenate([m[:n, n:], m[n:, n:]], axis=1),
        ],
        axis=0,
    )


def stack(m):
    return jnp.concatenate([m[:, :LANES], m[:, LANES:]], axis=0)


def tables(extent):
    counter = np.arange(extent)
    angles = (counter[:, None] * counter[None, :] % extent).astype(np.float32) * np.float32(
        2.0 * math.pi / extent
    )
    c, s = np.cos(angles), np.sin(angles)
    fwd = np.block([[c, -s], [s, c]]).astype(np.float32)
    inv = np.block([[c, s], [-s, c]]).astype(np.float32)
    return jnp.asarray(fwd, F32).astype(BF), jnp.asarray(inv, F32).astype(BF)


def patch_steps(phases, mask, spec, observed, scale, tabs, emit):
    t1, t2, t1s, t2s = tabs
    g = LANES
    trig = [sincos(p) for p in phases]
    cos = jnp.concatenate([c * mask for s, c in trig], axis=1)
    sin = jnp.concatenate([s * mask for s, c in trig], axis=1)
    x = swap_blocks(jnp.concatenate([cos.astype(BF), sin.astype(BF)], axis=0))
    y = dot(x, t1)
    yield
    focal = dot(t2, swap_blocks(y.astype(BF)))
    yield
    fr, fi = focal[:g], focal[g:]
    spread = (fr * fr + fi * fi) * scale
    y = dot(stack(spread.astype(BF)), t1[:g])
    yield
    otf = dot(t2, swap_blocks(y.astype(BF)))
    yield
    otr, oti = otf[:g], otf[g:]
    sr = jnp.concatenate([spec[:, :g]] * 2, axis=1)
    si = jnp.concatenate([spec[:, g:]] * 2, axis=1)
    mr = (sr * otr - si * oti).astype(BF)
    mi = (sr * oti + si * otr).astype(BF)
    y = dot(swap_blocks(jnp.concatenate([mr, mi], axis=0)), t2)
    yield
    image = dot(t1s[:g], swap_blocks(y.astype(BF)))
    yield
    obs = jnp.concatenate([o.astype(F32) for o in observed], axis=1)
    residual = image - obs
    y = dot(stack(residual.astype(BF)), t1[:g])
    yield
    grad = dot(t2s, swap_blocks(y.astype(BF)))
    yield
    gr, gi = grad[:g], grad[g:]
    ar = (gr * otr + gi * oti).astype(BF)
    ai = (gi * otr - gr * oti).astype(BF)
    half = dot(swap_blocks(jnp.concatenate([ar, ai], axis=0)), t2)
    br = (gr * sr + gi * si).astype(BF)
    bi = (gi * sr - gr * si).astype(BF)
    y = dot(swap_blocks(jnp.concatenate([br, bi], axis=0)), t2)
    yield
    term = dot(t1[:g], stack((half[:g] + half[g:]).astype(BF)))
    spread_grad = dot(t1[:g], swap_blocks(y.astype(BF)))
    yield
    factor = (2.0 * scale) * spread_grad
    fr, fi = (factor * fr).astype(BF), (factor * fi).astype(BF)
    y = dot(swap_blocks(jnp.concatenate([fr, fi], axis=0)), t2)
    yield
    field = dot(t1, swap_blocks(y.astype(BF)))
    yield
    emit(term, (field[g:] * cos - field[:g] * sin).astype(BF))


def interleave(work, lag):
    waiting, running, tick = list(work), [], 0
    while waiting or running:
        if waiting and tick % lag == 0:
            running.append(waiting.pop(0))
        running = [w for w in running if next(w, "done") is None]
        tick += 1


def kernel(
    sizes,
    coeff_in,
    object_in,
    mask_in,
    fwd_in,
    inv_in,
    expand_in,
    fold_in,
    observed_hbm,
    basis_hbm,
    coeff_out,
    object_out,
    basis,
    observed,
    spread_rows,
    phase,
    spectrum,
    slopes,
    wide,
    ag_send,
    ag_recv,
    rs_send,
    rs_recv,
    sc_send,
    sc_mid,
    sc_recv_frame,
    sc_recv_patch,
    load_sem,
    ag_sem,
    rs_sem,
    sc_sem,
):
    frames, patches, modes, n_frame, n_patch, rows = sizes
    g = LANES
    pairs = frames * patches
    groups = -(-modes // BLK)
    blocks = g // BLK
    me = lax.axis_index("frame")
    my_patch = lax.axis_index("patch")

    load_basis = pltpu.make_async_copy(basis_hbm, basis.at[pl.ds(0, modes)], load_sem.at[0])
    load_observed = pltpu.make_async_copy(observed_hbm, observed, load_sem.at[1])
    load_basis.start()
    load_observed.start()

    barrier = pltpu.get_barrier_semaphore()
    for k in range(1, n_frame):
        peer = lax.rem(me + k, n_frame)
        pl.semaphore_signal(barrier, inc=1, device_id={"frame": peer}, device_id_type=MESH)
    for k in range(1, n_patch):
        peer = lax.rem(my_patch + k, n_patch)
        pl.semaphore_signal(barrier, inc=1, device_id={"patch": peer}, device_id_type=MESH)

    object_out[...] = object_in[...]
    coeff_out[...] = coeff_in[...]
    ag_send[...] = object_in[...].astype(BF)
    if groups * BLK > modes:
        basis[pl.ds(modes, groups * BLK - modes)] = jnp.zeros((groups * BLK - modes, g, g), BF)
    mask = mask_in[...].astype(F32)
    scale = 1.0 / (g * g * jnp.sum(mask))
    sc_send[...] = jnp.zeros(sc_send.shape, F32)
    pl.semaphore_wait(barrier, n_frame + n_patch - 2)

    def gather(start):
        for k in range(1, n_frame):
            copy = pltpu.make_async_remote_copy(
                src_ref=ag_send,
                dst_ref=ag_recv.at[me],
                send_sem=ag_sem.at[0],
                recv_sem=ag_sem.at[1],
                device_id={"frame": lax.rem(me + k, n_frame)},
                device_id_type=MESH,
            )
            copy.start()

    def all_of(buffer, out, sem, axis, count):
        return pltpu.make_async_remote_copy(
            src_ref=out.at[pl.ds(0, count)],
            dst_ref=buffer.at[pl.ds(0, count)],
            send_sem=sem.at[0],
            recv_sem=sem.at[1],
            device_id={axis: 0},
            device_id_type=MESH,
        )

    row_of = lax.rem(lax.broadcasted_iota(jnp.int32, (BLK, 2 * g), 0), BLK)
    lane_of = lax.rem(lax.broadcasted_iota(jnp.int32, (BLK, 2 * g), 1), BLK)
    diagonal = row_of == lane_of

    def phase_maps():
        wide[...] = dot(coeff_out[...].astype(BF), expand_in[...])

        def spread_group(at, carry):
            values = wide[pl.ds(pl.multiple_of(at * pairs, pairs), pairs), :]
            values = jnp.broadcast_to(values[:, None, :], (pairs, BLK, 2 * g))
            values = jnp.where(diagonal[None], values, 0.0).astype(BF)
            spread_rows[at] = values.reshape(pairs * BLK, 2 * g)
            return carry

        lax.fori_loop(0, groups, spread_group, 0)

    def phase_products():
        lhs = jnp.concatenate([spread_rows[k] for k in range(groups)], axis=1)

        def block(at, carry):
            first = pl.multiple_of(at * 2 * BLK, 2 * BLK)
            depth = groups * BLK * BLK
            rhs = jnp.concatenate(
                [
                    basis[:, pl.ds(first, BLK), :].reshape(depth, g),
                    basis[:, pl.ds(first + BLK, BLK), :].reshape(depth, g),
                ],
                axis=1,
            )
            out = dot(lhs, rhs)
            phase[:, pl.ds(first, BLK), :] = out[:, :g].reshape(pairs, BLK, g)
            phase[:, pl.ds(first + BLK, BLK), :] = out[:, g:].reshape(pairs, BLK, g)
            return carry

        lax.fori_loop(0, blocks // 2, block, 0)

    def spectra():
        for q in range(0, patches, 2):
            pieces = [
                ag_recv[:, q + u].astype(F32).reshape(g, g).astype(BF) for u in range(2)
            ]
            left = dot(inv_in[:, :g], jnp.concatenate(pieces, axis=1))
            out = dot(swap_blocks(left.astype(BF)), fwd_in[...])
            spectrum[q] = out[:g]
            spectrum[q + 1] = out[g:]

    inverse = 1.0 / (g * g)

    def patch_chunk(at, carry):
        fwd, inv = fwd_in[...], inv_in[...]
        tabs = (fwd, inv, fwd * BF(inverse), inv * BF(inverse))

        def one(q):
            def emit(term, slope):
                rs_send[:, q] = term.reshape(n_frame, rows, g).astype(BF)
                for f in range(frames):
                    for b in range(blocks):
                        slopes[f * patches + q, :, pl.ds(b * g, g)] = slope[
                            b * BLK : (b + 1) * BLK, f * g : (f + 1) * g
                        ]

            picks = [f * patches + q for f in range(frames)]
            return patch_steps(
                [phase[p] for p in picks],
                mask,
                spectrum[q],
                [observed[p] for p in picks],
                scale,
                tabs,
                emit,
            )

        interleave([one(at * CHUNK + u) for u in range(CHUNK)], 1)
        for k in range(1, n_frame):
            peer = lax.rem(me + k, n_frame)
            part = pl.ds(pl.multiple_of(at * CHUNK, CHUNK), CHUNK)
            copy = pltpu.make_async_remote_copy(
                src_ref=rs_send.at[peer, part],
                dst_ref=rs_recv.at[me, part],
                send_sem=rs_sem.at[0],
                recv_sem=rs_sem.at[1],
                device_id={"frame": peer},
                device_id_type=MESH,
            )
            copy.start()
        return carry

    def coeff_products():
        lhs = slopes[...].reshape(pairs * BLK, blocks * g)

        def group(at, carry):
            first = pl.multiple_of(at * BLK, BLK)
            rhs = jnp.concatenate(
                [
                    basis[pl.ds(first, BLK), b * BLK : (b + 1) * BLK, :].reshape(BLK * BLK, g)
                    for b in range(blocks)
                ],
                axis=1,
            )
            out = lax.dot_general(lhs, rhs, (((1,), (1,)), ((), ())), preferred_element_type=F32)
            out = out.reshape(pairs, BLK, BLK * BLK)
            out = jnp.where(diagonal[None], out, 0.0)
            wide[pl.ds(pl.multiple_of(at * pairs, pairs), pairs), :] = jnp.sum(out, axis=1)
            return carry

        lax.fori_loop(0, groups, group, 0)
        rest, total = wide[...], 0.0
        for part in range(3):
            low = rest.astype(BF)
            total = total + dot(low, fold_in[...])
            rest = rest - low.astype(F32)
        return total

    def exchange(axis, count, own, send, recv, sem):
        for k in range(1, count):
            copy = pltpu.make_async_remote_copy(
                src_ref=send,
                dst_ref=recv.at[own],
                send_sem=sem.at[0],
                recv_sem=sem.at[1],
                device_id={axis: lax.rem(own + k, count)},
                device_id_type=MESH,
            )
            copy.start()

    for iteration in range(ITERS):
        gather(iteration)
        ag_recv[me] = ag_send[...]
        phase_maps()
        if iteration == 0:
            load_basis.wait()
        phase_products()
        both = all_of(ag_recv, ag_recv, ag_sem, "frame", n_frame - 1)
        both.wait_recv()
        both.wait_send()
        spectra()
        if iteration == 0:
            load_observed.wait()
        lax.fori_loop(0, patches // CHUNK, patch_chunk, 0)
        coeff_grad = coeff_products()
        both = all_of(rs_recv, rs_send, rs_sem, "frame", n_frame - 1)
        both.wait_recv()
        own_grad = rs_send[me].astype(F32)
        for k in range(1, n_frame):
            own_grad = own_grad + rs_recv[lax.rem(me + k, n_frame)].astype(F32)
        both.wait_send()

        sc_send[0:1, :] = jnp.sum(jnp.sum(own_grad * own_grad, axis=0), axis=0, keepdims=True)
        sc_send[1:2, 0:BLK] = jnp.sum(coeff_grad * coeff_grad, axis=0, keepdims=True)
        exchange("frame", n_frame, me, sc_send, sc_recv_frame, sc_sem.at[0])
        both = all_of(sc_recv_frame, sc_recv_frame, sc_sem.at[0], "frame", n_frame - 1)
        both.wait_recv()
        both.wait_send()
        total = sc_send[...]
        for k in range(1, n_frame):
            total = total + sc_recv_frame[lax.rem(me + k, n_frame)]
        sc_mid[...] = total
        from_patch = sc_recv_patch.at[iteration]
        exchange("patch", n_patch, my_patch, sc_mid, from_patch, sc_sem.at[1 + iteration])
        both = all_of(from_patch, from_patch, sc_sem.at[1 + iteration], "patch", n_patch - 1)
        both.wait_recv()
        both.wait_send()
        for k in range(1, n_patch):
            total = total + from_patch[lax.rem(my_patch + k, n_patch)]
        object_count = patches * rows * g * n_frame * n_patch
        coeff_count = pairs * modes * n_frame * n_patch
        object_rms = jnp.sqrt(jnp.sum(total[0:1], keepdims=True) / object_count + EPSILON)
        coeff_rms = jnp.sqrt(jnp.sum(total[1:2], keepdims=True) / coeff_count + EPSILON)
        coeff_out[...] = coeff_out[...] - STEP_COEFF * coeff_grad / coeff_rms
        updated = object_out[...] - STEP_OBJECT * own_grad / object_rms[None]
        object_out[...] = updated
        if iteration + 1 < ITERS:
            ag_send[...] = updated.astype(BF)


def local(n_frame, n_patch, coeffs, observed, object_field, mode_basis, pupil_mask):
    frames, patches, modes = coeffs.shape
    rows, g = object_field.shape[1:]
    pairs = frames * patches
    groups = -(-modes // BLK)
    padded = groups * BLK
    wide_in = jnp.pad(coeffs.reshape(pairs, modes), ((0, 0), (0, padded - modes)))
    wide_in = wide_in.reshape(pairs, groups, BLK).transpose(1, 0, 2).reshape(groups * pairs, BLK)
    fwd, inv = tables(g)
    expand = np.kron(np.eye(BLK), np.ones((1, BLK)))
    vmem = pl.BlockSpec(memory_space=pltpu.VMEM)
    hbm = pl.BlockSpec(memory_space=pl.ANY)
    dma = pltpu.SemaphoreType.DMA
    sizes = (frames, patches, modes, n_frame, n_patch, rows)
    new_coeffs, new_object = pl.pallas_call(
        functools.partial(kernel, sizes),
        out_shape=[
            jax.ShapeDtypeStruct((groups * pairs, BLK), F32),
            jax.ShapeDtypeStruct(object_field.shape, F32),
        ],
        in_specs=[vmem] * 7 + [hbm] * 2,
        out_specs=[vmem, vmem],
        scratch_shapes=[
            pltpu.VMEM((padded, g, g), BF),
            pltpu.VMEM((pairs, g, g), BF),
            pltpu.VMEM((groups, pairs * BLK, 2 * g), BF),
            pltpu.VMEM((pairs, g, g), F32),
            pltpu.VMEM((patches, g, 2 * g), F32),
            pltpu.VMEM((pairs, BLK, g * g // BLK), BF),
            pltpu.VMEM((groups * pairs, 2 * g), F32),
            pltpu.VMEM((patches, rows, g), BF),
            pltpu.VMEM((n_frame, patches, rows, g), BF),
            pltpu.VMEM((n_frame, patches, rows, g), BF),
            pltpu.VMEM((n_frame, patches, rows, g), BF),
            pltpu.VMEM((8, g), F32),
            pltpu.VMEM((8, g), F32),
            pltpu.VMEM((n_frame, 8, g), F32),
            pltpu.VMEM((ITERS, n_patch, 8, g), F32),
            dma((2,)),
            dma((2,)),
            dma((2,)),
            dma((1 + ITERS, 2)),
        ],
        compiler_params=pltpu.CompilerParams(
            collective_id=0, has_side_effects=True, vmem_limit_bytes=62 * 1024 * 1024
        ),
    )(
        wide_in,
        object_field,
        pupil_mask,
        fwd,
        inv,
        jnp.asarray(expand, BF),
        jnp.asarray(expand.T, BF),
        observed.reshape(pairs, g, g),
        mode_basis,
    )
    new_coeffs = new_coeffs.reshape(groups, pairs, BLK).transpose(1, 0, 2).reshape(pairs, padded)
    return new_coeffs[:, :modes].reshape(coeffs.shape), new_object


def solution(mesh):
    in_specs = (
        P("frame", "patch", None),
        P("frame", "patch", None, None),
        P("patch", "frame", None),
        P(),
        P(),
    )
    out_specs = (P("frame", "patch", None), P("patch", "frame", None))
    run = functools.partial(local, mesh.shape["frame"], mesh.shape["patch"])
    return jax.shard_map(run, mesh=mesh, in_specs=in_specs, out_specs=out_specs, check_vma=False)
```

time: 622 us -> 90.1 us (0.14)
  matrix products: 194 us -> 0 us
  blocking collectives: 179 us -> 0 us
  waiting for transfers between devices: 157 us -> 0 us
  Pallas kernels: 0 us -> 84.1 us
  local copies, waits for them, and re-layouts: 57.8 us -> 5.1 us
  between operations: 18.5 us -> 0.65 us
  other arithmetic: 10.7 us -> 0 us
    dot_general x100 -> x0, matrix products: 194 us -> none  [the longest x40 85 us: left_mul(): jnp.einsum('jb,nbk->njk', matrix, values, preferred_element_type=jnp.floa...]
    psum x2 -> x0, waiting for transfers between devices: 157 us -> none  [shards(): lax.psum((full_real - full_imag).astype(jnp.bfloat16), 'frame')]
    psum x2 -> x0, blocking collectives: 134 us -> none  [shards(): lax.psum((jnp.sum(own_grad * own_grad), jnp.sum(coeff_grad * coeff_grad))...]
    pallas_call x0 -> x1, Pallas kernels: none -> 84.1 us  [local(): pl.pallas_call(functools.partial(kernel, sizes), out_shape=[jax.ShapeDtyp...]
    all_gather x2 -> x0, blocking collectives: 45.1 us -> none  [shards(): lax.all_gather(object_field.astype(jnp.bfloat16), 'frame', axis=1, tiled=...]
    dot_general x9 -> x0, local copies, waits for them, and re-layouts: 35.4 us -> none  [the longest x8 23.4 us: left_mul(): jnp.einsum('jb,nbk->njk', matrix, values, preferred_element_type=jnp.floa...]
    unnamed x74 -> x2, local copies, waits for them, and re-layouts: 10.5 us -> 2.37 us
  transfers between devices with their start and end apart: 2 -> 0, of which waited for: 2 -> 0; matrix products, arithmetic and copies ran while one was open for 12% -> 0% of each run, Pallas kernels for 0% -> 0%
where the time goes in v1:
time: 90.1 us; the launch traced here: 89.8 us
  Pallas kernels  84.1 us (93%)
  local copies, waits for them, and re-layouts  5.1 us (6%)
    pallas_call x1, Pallas kernels, local(): pl.pallas_call(functools.partial(kernel, sizes), out_shape=[jax.ShapeDtyp...  84.1 us
    unnamed x2, local copies, waits for them, and re-layouts  2.37 us

profile of v1, /device:TPU:1, one launch (start us, length us, event | category | flops | bytes accessed | tf_op | source)
XLA Modules:
  0.0 89.8 jit_solution(5620763561089170090)
XLA Ops:
  0.6 0.9 %copy.19 = f32[32,300]{0,1:T(8,128)S(1)} copy(f32[32,300]{1,0:T(8,128)} %bitcast.17) | data formatting | bytes 76800
  1.6 0.9 copy.16
  2.4 84.1 %shard_map.104 = (f32[608,16]{1,0:T(8,128)}, f32[16,8,128]{2,1,0:T(8,128)}) custom-call(f32[608,16]{1,0:T(8,128)} %bitcast.12, f32[16,8,128]{2,1,0:T(8,128)} %object_in.1, s32[128,128]{1,0:T(8,128)} %mask_in.1, bf16[256,256]{1,0:T(8,128)(2,1)} %constant.20.fwd_in, bf16[256,256]{1,0:T(8,128)(2,1)} %constant.21.inv_in, ...), custom_call_target="tpu_custom_call" | custom-call | tf_op jit(solution)/shard_map/pallas_call | solution.py:418
  86.5 1.1 %copy.17 = f32[19,32,16]{1,2,0:T(8,128)S(1)} copy(f32[19,32,16]{2,1,0:T(8,128)} %bitcast.16) | data formatting | bytes 77824 | tf_op jit(solution)/shard_map/reshape | solution.py:461
  87.6 0.7 copy.18
  88.4 1.5 %copy.21 = f32[16,8,128]{2,1,0:T(8,128)} copy(f32[16,8,128]{2,1,0:T(8,128)} %get-tuple-element.11) | data formatting | bytes 131072
  (1 shorter events, 0.0 us)

commit v2 on v1

v2 whole, which is shorter than its diff:
```python
import functools
import math

import jax
import jax.numpy as jnp
import numpy as np
from jax import lax
from jax.experimental import pallas as pl
from jax.experimental.pallas import tpu as pltpu
from jax.sharding import PartitionSpec as P

EPSILON = 1e-06
STEP_OBJECT = 0.1
STEP_COEFF = 0.2
CHUNK = 8
BLK = 8
PARTS = 10
LANES = 128
MESH = pl.DeviceIdType.MESH
BF = jnp.bfloat16
F32 = jnp.float32


def fit(even):
    f = np.cos((np.arange(4000) + 0.5) * (np.pi / 8000)) * 0.5
    target = np.sqrt(2.0) * (np.cos(np.pi * f) if even else np.sin(np.pi * f) / f)
    powers = np.stack([f ** (2 * k) for k in range(6 if even else 5)], axis=1)
    coef = np.linalg.lstsq(powers, target, rcond=None)[0]
    return [float(np.float32(v)) for v in coef]


SIN_COEF = fit(False)
COS_COEF = fit(True)


def horner(z, coef):
    acc = coef[-1] * z + coef[-2]
    for value in coef[-3::-1]:
        acc = acc * z + value
    return acc


def sincos(x):
    turns = x * (1.0 / (2.0 * math.pi))
    f = turns - jnp.round(turns)
    z = f * f
    s = f * horner(z, SIN_COEF)
    c = horner(z, COS_COEF)
    return s * c, 1.0 - s * s


def dot(a, b):
    return jnp.dot(a, b, preferred_element_type=F32)


def swap_blocks(m):
    n = LANES
    return jnp.concatenate(
        [
            jnp.concatenate([m[:n, :n], m[n:, :n]], axis=1),
            jnp.concatenate([m[:n, n:], m[n:, n:]], axis=1),
        ],
        axis=0,
    )


def stack(m):
    return jnp.concatenate([m[:, :LANES], m[:, LANES:]], axis=0)


def tables(extent):
    counter = np.arange(extent)
    angles = (counter[:, None] * counter[None, :] % extent).astype(np.float32) * np.float32(
        2.0 * math.pi / extent
    )
    c, s = np.cos(angles), np.sin(angles)
    fwd = np.block([[c, -s], [s, c]]).astype(np.float32)
    inv = np.block([[c, s], [-s, c]]).astype(np.float32)
    return jnp.asarray(fwd, F32).astype(BF), jnp.asarray(inv, F32).astype(BF)


def patch_steps(phases, mask, spec, observed, scale, tabs, emit):
    t1, t2, t1s, t2s = tabs
    g = LANES
    trig = [sincos(p) for p in phases]
    cos = jnp.concatenate([c * mask for s, c in trig], axis=1)
    sin = jnp.concatenate([s * mask for s, c in trig], axis=1)
    x = swap_blocks(jnp.concatenate([cos.astype(BF), sin.astype(BF)], axis=0))
    y = dot(x, t1)
    yield
    focal = dot(t2, swap_blocks(y.astype(BF)))
    yield
    fr, fi = focal[:g], focal[g:]
    spread = (fr * fr + fi * fi) * scale
    y = dot(stack(spread.astype(BF)), t1[:g])
    yield
    otf = dot(t2, swap_blocks(y.astype(BF)))
    yield
    otr, oti = otf[:g], otf[g:]
    sr = jnp.concatenate([spec[:, :g]] * 2, axis=1)
    si = jnp.concatenate([spec[:, g:]] * 2, axis=1)
    mr = (sr * otr - si * oti).astype(BF)
    mi = (sr * oti + si * otr).astype(BF)
    y = dot(swap_blocks(jnp.concatenate([mr, mi], axis=0)), t2)
    yield
    image = dot(t1s[:g], swap_blocks(y.astype(BF)))
    yield
    obs = jnp.concatenate([o.astype(F32) for o in observed], axis=1)
    residual = image - obs
    y = dot(stack(residual.astype(BF)), t1[:g])
    yield
    grad = dot(t2s, swap_blocks(y.astype(BF)))
    yield
    gr, gi = grad[:g], grad[g:]
    ar = (gr * otr + gi * oti).astype(BF)
    ai = (gi * otr - gr * oti).astype(BF)
    half = dot(swap_blocks(jnp.concatenate([ar, ai], axis=0)), t2)
    br = (gr * sr + gi * si).astype(BF)
    bi = (gi * sr - gr * si).astype(BF)
    y = dot(swap_blocks(jnp.concatenate([br, bi], axis=0)), t2)
    yield
    term = dot(t1[:g], stack((half[:g] + half[g:]).astype(BF)))
    spread_grad = dot(t1[:g], swap_blocks(y.astype(BF)))
    yield
    factor = (2.0 * scale) * spread_grad
    fr, fi = (factor * fr).astype(BF), (factor * fi).astype(BF)
    y = dot(swap_blocks(jnp.concatenate([fr, fi], axis=0)), t2)
    yield
    field = dot(t1, swap_blocks(y.astype(BF)))
    yield
    emit(term, field[g:] * cos - field[:g] * sin)


def interleave(work, lag):
    waiting, running, tick = list(work), [], 0
    while waiting or running:
        if waiting and tick % lag == 0:
            running.append(waiting.pop(0))
        running = [w for w in running if next(w, "done") is None]
        tick += 1


def kernel(
    sizes,
    coeff_in,
    object_in,
    mask_in,
    fwd_in,
    inv_in,
    expand_in,
    fold_in,
    observed_hbm,
    basis_hbm,
    coeff_out,
    object_out,
    staged,
    basis,
    observed,
    rows_left,
    phase,
    phase_step,
    spectrum,
    slopes,
    wide,
    coeff_now,
    turned,
    kept,
    ag_send,
    ag_recv,
    rs_send,
    rs_recv,
    sc_send,
    sc_mid,
    sc_frame,
    sc_patch,
    basis_sem,
    load_sem,
    ag_sem,
    rs_sem,
    sc_sem,
):
    frames, patches, modes, n_frame, n_patch, rows = sizes
    g = LANES
    pairs = frames * patches
    blocks = g // BLK
    depth = modes * BLK
    span = 2 * g
    groups = -(-depth // span)
    lane_blocks = -(-modes // g)
    part = modes // PARTS
    me = lax.axis_index("frame")
    my_patch = lax.axis_index("patch")

    loads = [
        pltpu.make_async_copy(
            basis_hbm.at[pl.ds(k * part, part)], staged.at[pl.ds(k * part, part)], basis_sem.at[k]
        )
        for k in range(PARTS)
    ]
    for load in loads:
        load.start()
    load_observed = pltpu.make_async_copy(observed_hbm, observed, load_sem)
    load_observed.start()

    barrier = pltpu.get_barrier_semaphore()
    for k in range(1, n_frame):
        peer = lax.rem(me + k, n_frame)
        pl.semaphore_signal(barrier, inc=1, device_id={"frame": peer}, device_id_type=MESH)
    for k in range(1, n_patch):
        peer = lax.rem(my_patch + k, n_patch)
        pl.semaphore_signal(barrier, inc=1, device_id={"patch": peer}, device_id_type=MESH)

    ag_send[0] = object_in[...].astype(BF)
    coeff_now[...] = jnp.zeros(coeff_now.shape, F32)
    coeff_now[:, 0:modes] = coeff_in[...]
    wide[...] = jnp.zeros(wide.shape, F32)
    basis[:, pl.ds(depth, groups * span - depth), :] = jnp.zeros(
        (blocks, groups * span - depth, g), BF
    )
    mask = mask_in[...].astype(F32)
    scale = 1.0 / (g * g * jnp.sum(mask))
    sc_send[...] = jnp.zeros(sc_send.shape, F32)

    def gather(at):
        for k in range(1, n_frame):
            copy = pltpu.make_async_remote_copy(
                src_ref=ag_send.at[at],
                dst_ref=ag_recv.at[at, me],
                send_sem=ag_sem.at[at, 0],
                recv_sem=ag_sem.at[at, 1],
                device_id={"frame": lax.rem(me + k, n_frame)},
                device_id_type=MESH,
            )
            copy.start()

    def all_of(buffer, out, sem, axis, count):
        return pltpu.make_async_remote_copy(
            src_ref=out.at[pl.ds(0, count)],
            dst_ref=buffer.at[pl.ds(0, count)],
            send_sem=sem.at[0],
            recv_sem=sem.at[1],
            device_id={axis: 0},
            device_id_type=MESH,
        )

    row_of = lax.broadcasted_iota(jnp.int32, (BLK, span), 0)
    lane_of = lax.rem(lax.broadcasted_iota(jnp.int32, (BLK, span), 1), BLK)
    diagonal = row_of == lane_of

    def left_rows(pieces):
        for k in range(lane_blocks):
            width = min(groups * span - k * g * BLK, g * BLK)
            values = dot(pieces[k].astype(BF), expand_in[:, :width])
            for b in range(width // span):
                cut = values[:, b * span : (b + 1) * span]
                cut = jnp.broadcast_to(cut[:, None, :], (pairs, BLK, span))
                cut = jnp.where(diagonal[None], cut, 0.0)
                first = k * g * BLK + b * span
                rows_left[:, first : first + span] = cut.reshape(pairs * BLK, span).astype(BF)

    def basis_products(out_ref, start, stop):
        lhs = rows_left[:, :depth]

        def block(at, carry):
            rhs = jnp.concatenate([basis[2 * at, :depth, :], basis[2 * at + 1, :depth, :]], axis=1)
            out = dot(lhs, rhs)
            first = pl.multiple_of(at * 2 * BLK, 2 * BLK)
            out_ref[:, pl.ds(first, BLK), :] = out[:, :g].reshape(pairs, BLK, g)
            out_ref[:, pl.ds(first + BLK, BLK), :] = out[:, g:].reshape(pairs, BLK, g)
            return carry

        lax.fori_loop(start, stop, block, 0, unroll=2)

    def relay(k):
        def block(b, carry):
            taken = staged[pl.ds(k * part, part), pl.ds(pl.multiple_of(b * 2 * BLK, 2 * BLK), 2 * BLK), :]
            taken = taken.astype(F32)
            for h in range(2):
                half = taken[:, h * BLK : (h + 1) * BLK].reshape(part * BLK, g)
                basis[2 * b + h, pl.ds(k * part * BLK, part * BLK), :] = half.astype(BF)
            return carry

        lax.fori_loop(0, blocks // 2, block, 0)

    def spectra(rows_of):
        for q in range(0, patches, 2):
            pieces = [rows_of(q + u).reshape(g, g).astype(BF) for u in range(2)]
            left = dot(inv_in[:, :g], jnp.concatenate(pieces, axis=1))
            out = dot(swap_blocks(left.astype(BF)), fwd_in[...])
            spectrum[q] = out[:g]
            spectrum[q + 1] = out[g:]

    inverse = 1.0 / (g * g)

    def patch_chunk(phase_of, at, carry):
        fwd, inv = fwd_in[...], inv_in[...]
        tabs = (fwd, inv, fwd * BF(inverse), inv * BF(inverse))

        def one(q):
            def emit(term, slope):
                rs_send[:, q] = term.reshape(n_frame, rows, g).astype(BF)
                first = pl.multiple_of(q * frames * BLK, frames * BLK)
                for b in range(blocks):
                    cut = slope[b * BLK : (b + 1) * BLK]
                    cut = jnp.concatenate([cut[:, f * g : (f + 1) * g] for f in range(frames)], axis=0)
                    slopes[pl.ds(first, frames * BLK), b * g : (b + 1) * g] = cut.astype(BF)

            picks = [f * patches + q for f in range(frames)]
            return patch_steps(
                [phase_of(p) for p in picks],
                mask,
                spectrum[q],
                [observed[p] for p in picks],
                scale,
                tabs,
                emit,
            )

        interleave([one(at * CHUNK + u) for u in range(CHUNK)], 1)
        for k in range(1, n_frame):
            peer = lax.rem(me + k, n_frame)
            some = pl.ds(pl.multiple_of(at * CHUNK, CHUNK), CHUNK)
            copy = pltpu.make_async_remote_copy(
                src_ref=rs_send.at[peer, some],
                dst_ref=rs_recv.at[me, some],
                send_sem=rs_sem.at[0],
                recv_sem=rs_sem.at[1],
                device_id={"frame": peer},
                device_id_type=MESH,
            )
            copy.start()
        return carry

    def coeff_products():
        lhs = slopes[...]

        def group(at, carry):
            first = pl.multiple_of(at * span, span)
            rhs = jnp.concatenate([basis[b, pl.ds(first, span), :] for b in range(blocks)], axis=1)
            out = lax.dot_general(lhs, rhs, (((1,), (1,)), ((), ())), preferred_element_type=F32)
            out = jnp.where(diagonal[None], out.reshape(pairs, BLK, span), 0.0)
            wide[at] = jnp.sum(out, axis=1)
            return carry

        lax.fori_loop(0, groups, group, 0, unroll=2)
        per = g * BLK // span
        rest = jnp.concatenate(
            [
                jnp.concatenate([wide[k * per + b] for b in range(per)], axis=1)
                for k in range(lane_blocks)
            ],
            axis=0,
        )
        total = 0.0
        for _ in range(3):
            low = rest.astype(BF)
            total = total + dot(low, fold_in[...])
            rest = rest - low.astype(F32)
        pieces = []
        for k in range(lane_blocks):
            turned[k] = total[k * pairs : (k + 1) * pairs]
            pieces.append(
                jnp.concatenate(
                    [turned[k, pl.ds(f, patches, stride=frames), :] for f in range(frames)], axis=0
                )
            )
        return pieces

    def exchange(axis, count, own, send, recv, sem):
        for k in range(1, count):
            copy = pltpu.make_async_remote_copy(
                src_ref=send,
                dst_ref=recv.at[own],
                send_sem=sem.at[0],
                recv_sem=sem.at[1],
                device_id={axis: lax.rem(own + k, count)},
                device_id_type=MESH,
            )
            copy.start()

    def frame_sum():
        both = all_of(sc_frame, sc_frame, sc_sem.at[0], "frame", n_frame - 1)
        both.wait_recv()
        both.wait_send()
        total = sc_send[...]
        for k in range(1, n_frame):
            total = total + sc_frame[lax.rem(me + k, n_frame)]
        sc_mid[...] = total

    def patch_sum(at):
        recv, sem = sc_patch.at[at], sc_sem.at[1 + at]
        both = all_of(recv, recv, sem, "patch", n_patch - 1)
        both.wait_recv()
        both.wait_send()
        total = sc_mid[...]
        for k in range(1, n_patch):
            total = total + recv[lax.rem(my_patch + k, n_patch)]
        object_count = patches * rows * g * n_frame * n_patch
        coeff_count = pairs * modes * n_frame * n_patch
        object_rms = jnp.sqrt(jnp.sum(total[0:1], keepdims=True) / object_count + EPSILON)
        coeff_rms = jnp.sqrt(jnp.sum(total[1:2], keepdims=True) / coeff_count + EPSILON)
        return STEP_OBJECT / object_rms, STEP_COEFF / coeff_rms

    def finish_iteration():
        pieces = coeff_products()
        both = all_of(rs_recv, rs_send, rs_sem, "frame", n_frame - 1)
        both.wait_recv()
        own = rs_send[me].astype(F32)
        for k in range(1, n_frame):
            own = own + rs_recv[lax.rem(me + k, n_frame)].astype(F32)
        both.wait_send()
        sc_send[0:1, :] = jnp.sum(jnp.sum(own * own, axis=0), axis=0, keepdims=True)
        squares = sum(piece * piece for piece in pieces)
        sc_send[1:2, :] = jnp.sum(squares, axis=0, keepdims=True)
        return pieces, own

    halfway = blocks // 4

    left_rows([coeff_now[:, k * g : (k + 1) * g] for k in range(lane_blocks)])
    pl.semaphore_wait(barrier, n_frame + n_patch - 2)
    gather(0)
    ag_recv[0, me] = ag_send[0]
    for k in range(PARTS):
        loads[k].wait()
        relay(k)
    basis_products(phase, 0, blocks // 2)
    both = all_of(ag_recv.at[0], ag_recv.at[0], ag_sem.at[0], "frame", n_frame - 1)
    both.wait_recv()
    both.wait_send()
    spectra(lambda q: ag_recv[0, :, q].astype(F32))
    load_observed.wait()
    lax.fori_loop(0, patches // CHUNK, functools.partial(patch_chunk, lambda p: phase[p]), 0)
    pieces, own = finish_iteration()
    ag_send[1] = own.astype(BF)
    exchange("frame", n_frame, me, sc_send, sc_frame, sc_sem.at[0])

    left_rows(pieces)
    gather(1)
    ag_recv[1, me] = ag_send[1]
    for k in range(lane_blocks):
        kept[k] = pieces[k]
    object_out[...] = own
    basis_products(phase_step, 0, halfway)
    frame_sum()
    exchange("patch", n_patch, my_patch, sc_mid, sc_patch.at[0], sc_sem.at[1])
    basis_products(phase_step, halfway, blocks // 2)
    object_step, coeff_step = patch_sum(0)
    object_out[...] = object_in[...] - object_step[None] * object_out[...]
    for k in range(lane_blocks):
        cut = slice(k * g, (k + 1) * g)
        coeff_now[:, cut] = coeff_now[:, cut] - coeff_step * kept[k]
    both = all_of(ag_recv.at[1], ag_recv.at[1], ag_sem.at[1], "frame", n_frame - 1)
    both.wait_recv()
    both.wait_send()

    spectra(
        lambda q: ag_recv[0, :, q].astype(F32) - object_step[None] * ag_recv[1, :, q].astype(F32)
    )
    lax.fori_loop(
        0,
        patches // CHUNK,
        functools.partial(patch_chunk, lambda p: phase[p] - coeff_step * phase_step[p]),
        0,
    )
    pieces, own = finish_iteration()
    exchange("frame", n_frame, me, sc_send, sc_frame, sc_sem.at[0])
    frame_sum()
    exchange("patch", n_patch, my_patch, sc_mid, sc_patch.at[1], sc_sem.at[2])
    object_step, coeff_step = patch_sum(1)
    object_out[...] = object_out[...] - object_step[None] * own
    for k in range(lane_blocks):
        width = min(g, modes - k * g)
        cut = slice(k * g, k * g + width)
        coeff_out[:, cut] = coeff_now[:, cut] - coeff_step * pieces[k][:, :width]


def local(n_frame, n_patch, coeffs, observed, object_field, mode_basis, pupil_mask):
    frames, patches, modes = coeffs.shape
    rows, g = object_field.shape[1:]
    pairs = frames * patches
    blocks = g // BLK
    span = 2 * g
    padded = -(-modes * BLK // span) * span
    lane_blocks = -(-modes // g)
    fwd, inv = tables(g)
    expand = np.kron(np.eye(g), np.ones((1, BLK)))
    vmem = pl.BlockSpec(memory_space=pltpu.VMEM)
    hbm = pl.BlockSpec(memory_space=pl.ANY)
    dma = pltpu.SemaphoreType.DMA
    sizes = (frames, patches, modes, n_frame, n_patch, rows)
    new_coeffs, new_object = pl.pallas_call(
        functools.partial(kernel, sizes),
        out_shape=[
            jax.ShapeDtypeStruct((pairs, modes), F32),
            jax.ShapeDtypeStruct(object_field.shape, F32),
        ],
        in_specs=[vmem] * 7 + [hbm] * 2,
        out_specs=[vmem, vmem],
        scratch_shapes=[
            pltpu.VMEM((modes, g, g), BF),
            pltpu.VMEM((blocks, padded, g), BF),
            pltpu.VMEM((pairs, g, g), BF),
            pltpu.VMEM((pairs * BLK, padded), BF),
            pltpu.VMEM((pairs, g, g), F32),
            pltpu.VMEM((pairs, g, g), F32),
            pltpu.VMEM((patches, g, span), F32),
            pltpu.VMEM((pairs * BLK, blocks * g), BF),
            pltpu.VMEM((lane_blocks * g * BLK // span, pairs, span), F32),
            pltpu.VMEM((pairs, lane_blocks * g), F32),
            pltpu.VMEM((lane_blocks, pairs, g), F32),
            pltpu.VMEM((lane_blocks, pairs, g), F32),
            pltpu.VMEM((2, patches, rows, g), BF),
            pltpu.VMEM((2, n_frame, patches, rows, g), BF),
            pltpu.VMEM((n_frame, patches, rows, g), BF),
            pltpu.VMEM((n_frame, patches, rows, g), BF),
            pltpu.VMEM((8, g), F32),
            pltpu.VMEM((8, g), F32),
            pltpu.VMEM((n_frame, 8, g), F32),
            pltpu.VMEM((2, n_patch, 8, g), F32),
            dma((PARTS,)),
            dma(()),
            dma((2, 2)),
            dma((2,)),
            dma((3, 2)),
        ],
        compiler_params=pltpu.CompilerParams(
            collective_id=0, has_side_effects=True, vmem_limit_bytes=62 * 1024 * 1024
        ),
    )(
        coeffs.reshape(pairs, modes),
        object_field,
        pupil_mask,
        fwd,
        inv,
        jnp.asarray(expand, BF),
        jnp.asarray(expand.T, BF),
        observed.reshape(pairs, g, g),
        mode_basis,
    )
    return new_coeffs.reshape(coeffs.shape), new_object


def solution(mesh):
    in_specs = (
        P("frame", "patch", None),
        P("frame", "patch", None, None),
        P("patch", "frame", None),
        P(),
        P(),
    )
    out_specs = (P("frame", "patch", None), P("patch", "frame", None))
    run = functools.partial(local, mesh.shape["frame"], mesh.shape["patch"])
    return jax.shard_map(run, mesh=mesh, in_specs=in_specs, out_specs=out_specs, check_vma=False)
```

time: 90.1 us -> 73.5 us (0.82)
  Pallas kernels: 84.1 us -> 69.7 us
  local copies, waits for them, and re-layouts: 5.1 us -> 2.89 us
    pallas_call x1, Pallas kernels: 84.1 us -> 69.7 us  [local(): pl.pallas_call(functools.partial(kernel, sizes), out_shape=[jax.ShapeDtyp...]
    reshape x1 -> x0, local copies, waits for them, and re-layouts: 1.1 us -> none  [local(): new_coeffs.reshape(groups, pairs, BLK).transpose(1, 0, 2)]
where the time goes in v2:
time: 73.5 us; the launch traced here: 73.2 us
  Pallas kernels  69.7 us (95%)
  local copies, waits for them, and re-layouts  2.89 us (4%)
    pallas_call x1, Pallas kernels, local(): pl.pallas_call(functools.partial(kernel, sizes), out_shape=[jax.ShapeDtyp...  69.7 us
    unnamed x2, local copies, waits for them, and re-layouts  2.89 us

profile of v2, /device:TPU:1, one launch (start us, length us, event | category | flops | bytes accessed | tf_op | source)
XLA Modules:
  0.0 73.2 jit_solution(636796923360126346)
XLA Ops:
  0.6 69.7 %shard_map.104 = (f32[32,300]{1,0:T(8,128)}, f32[16,8,128]{2,1,0:T(8,128)}) custom-call(f32[32,300]{1,0:T(8,128)} %bitcast.4, f32[16,8,128]{2,1,0:T(8,128)} %object_in.1, s32[128,128]{1,0:T(8,128)} %mask_in.1, bf16[256,256]{1,0:T(8,128)(2,1)} %constant.15.fwd_in, bf16[256,256]{1,0:T(8,128)(2,1)} %constant.16.inv_in, ...), custom_call_target="tpu_custom_call" | custom-call | tf_op jit(solution)/shard_map/pallas_call | solution.py:491
  70.3 1.4 %copy.13 = f32[2,16,300]{2,1,0:T(8,128)} copy(f32[2,16,300]{2,1,0:T(8,128)} %bitcast.5) | data formatting | bytes 76800
  71.8 1.5 %copy.14 = f32[16,8,128]{2,1,0:T(8,128)} copy(f32[16,8,128]{2,1,0:T(8,128)} %get-tuple-element.9) | data formatting | bytes 131072

commit v3 on v2

v3 whole, which is shorter than its diff:
```python
import functools
import math

import jax
import jax.numpy as jnp
import numpy as np
from jax import lax
from jax.experimental import pallas as pl
from jax.experimental.pallas import tpu as pltpu
from jax.sharding import PartitionSpec as P

EPSILON = 1e-06
STEP_OBJECT = 0.1
STEP_COEFF = 0.2
CHUNK = 8
BLK = 8
PARTS = 10
LANES = 128
MESH = pl.DeviceIdType.MESH
BF = jnp.bfloat16
F32 = jnp.float32


def fit(even):
    f = np.cos((np.arange(4000) + 0.5) * (np.pi / 8000)) * 0.5
    target = np.sqrt(2.0) * (np.cos(np.pi * f) if even else np.sin(np.pi * f) / f)
    powers = np.stack([f ** (2 * k) for k in range(6 if even else 5)], axis=1)
    coef = np.linalg.lstsq(powers, target, rcond=None)[0]
    return [float(np.float32(v)) for v in coef]


SIN_COEF = fit(False)
COS_COEF = fit(True)


def horner(z, coef):
    acc = coef[-1] * z + coef[-2]
    for value in coef[-3::-1]:
        acc = acc * z + value
    return acc


def sincos(x):
    turns = x * (1.0 / (2.0 * math.pi))
    f = turns - jnp.round(turns)
    z = f * f
    s = f * horner(z, SIN_COEF)
    c = horner(z, COS_COEF)
    return s * c, 1.0 - s * s


def dot(a, b):
    return jnp.dot(a, b, preferred_element_type=F32)


def swap_blocks(m):
    n = LANES
    return jnp.concatenate(
        [
            jnp.concatenate([m[:n, :n], m[n:, :n]], axis=1),
            jnp.concatenate([m[:n, n:], m[n:, n:]], axis=1),
        ],
        axis=0,
    )


def stack(m):
    return jnp.concatenate([m[:, :LANES], m[:, LANES:]], axis=0)


def tables(extent):
    counter = np.arange(extent)
    angles = (counter[:, None] * counter[None, :] % extent).astype(np.float32) * np.float32(
        2.0 * math.pi / extent
    )
    c, s = np.cos(angles), np.sin(angles)
    fwd = np.block([[c, -s], [s, c]]).astype(np.float32)
    inv = np.block([[c, s], [-s, c]]).astype(np.float32)
    return jnp.asarray(fwd, F32).astype(BF), jnp.asarray(inv, F32).astype(BF)


def patch_steps(phases, mask, spec, observed, scale, tabs, emit_term, emit_slope):
    t1, t2, t1s, t2s = tabs
    g = LANES
    trig = [sincos(p) for p in phases]
    cos = jnp.concatenate([c * mask for s, c in trig], axis=1)
    sin = jnp.concatenate([s * mask for s, c in trig], axis=1)
    x = swap_blocks(jnp.concatenate([cos.astype(BF), sin.astype(BF)], axis=0))
    y = dot(x, t1)
    yield
    focal = dot(t2, swap_blocks(y.astype(BF)))
    yield
    fr, fi = focal[:g], focal[g:]
    spread = (fr * fr + fi * fi) * scale
    y = dot(stack(spread.astype(BF)), t1[:g])
    yield
    otf = dot(t2, swap_blocks(y.astype(BF)))
    yield
    otr, oti = otf[:g], otf[g:]
    sr = jnp.concatenate([spec[:, :g]] * 2, axis=1)
    si = jnp.concatenate([spec[:, g:]] * 2, axis=1)
    mr = (sr * otr - si * oti).astype(BF)
    mi = (sr * oti + si * otr).astype(BF)
    y = dot(swap_blocks(jnp.concatenate([mr, mi], axis=0)), t2)
    yield
    image = dot(t1s[:g], swap_blocks(y.astype(BF)))
    yield
    obs = jnp.concatenate([o.astype(F32) for o in observed], axis=1)
    residual = image - obs
    y = dot(stack(residual.astype(BF)), t1[:g])
    yield
    grad = dot(t2s, swap_blocks(y.astype(BF)))
    yield
    gr, gi = grad[:g], grad[g:]
    ar = (gr * otr + gi * oti).astype(BF)
    ai = (gi * otr - gr * oti).astype(BF)
    half = dot(swap_blocks(jnp.concatenate([ar, ai], axis=0)), t2)
    br = (gr * sr + gi * si).astype(BF)
    bi = (gi * sr - gr * si).astype(BF)
    y = dot(swap_blocks(jnp.concatenate([br, bi], axis=0)), t2)
    yield
    term = dot(t1[:g], stack((half[:g] + half[g:]).astype(BF)))
    spread_grad = dot(t1[:g], swap_blocks(y.astype(BF)))
    yield
    emit_term(term)
    factor = (2.0 * scale) * spread_grad
    fr, fi = (factor * fr).astype(BF), (factor * fi).astype(BF)
    y = dot(swap_blocks(jnp.concatenate([fr, fi], axis=0)), t2)
    yield
    field = dot(t1, swap_blocks(y.astype(BF)))
    yield
    emit_slope(field[g:] * cos - field[:g] * sin)


def interleave(work):
    waiting, running = list(work), []
    while waiting or running:
        running += waiting[:1]
        waiting = waiting[1:]
        running = [w for w in running if next(w, "done") is None]


def kernel(
    sizes,
    coeff_in,
    object_in,
    mask_in,
    fwd_in,
    inv_in,
    observed_hbm,
    basis_hbm,
    coeff_out,
    object_out,
    staged,
    basis,
    observed,
    rows_left,
    phase,
    phase_step,
    spectrum,
    slopes,
    wide,
    coeff_now,
    turned,
    kept,
    old,
    own_grad,
    expand,
    ag_send,
    ag_recv,
    rs_send,
    rs_recv,
    sc_send,
    sc_recv,
    steps,
    basis_sem,
    load_sem,
    ag_sem,
    rs_sem,
    sc_sem,
):
    frames, patches, modes, n_frame, n_patch, rows = sizes
    g = LANES
    pairs = frames * patches
    blocks = g // BLK
    depth = modes * BLK
    span = 2 * g
    groups = -(-depth // span)
    lane_blocks = -(-modes // g)
    part = modes // PARTS
    me = lax.axis_index("frame")
    my_patch = lax.axis_index("patch")

    loads = [
        pltpu.make_async_copy(
            basis_hbm.at[pl.ds(k * part, part)], staged.at[pl.ds(k * part, part)], basis_sem.at[k]
        )
        for k in range(PARTS)
    ]
    for load in loads:
        load.start()
    load_observed = pltpu.make_async_copy(observed_hbm, observed, load_sem)
    load_observed.start()

    others = [
        {"frame": lax.rem(me + k, n_frame), "patch": lax.rem(my_patch + m, n_patch)}
        for k in range(n_frame)
        for m in range(n_patch)
        if k or m
    ]
    barrier = pltpu.get_barrier_semaphore()
    for device in others:
        pl.semaphore_signal(barrier, inc=1, device_id=device, device_id_type=MESH)

    ag_send[0] = object_in[...].astype(BF)
    coeff_now[...] = jnp.zeros(coeff_now.shape, F32)
    coeff_now[:, 0:modes] = coeff_in[...]
    wide[...] = jnp.zeros(wide.shape, F32)
    basis[:, pl.ds(depth, groups * span - depth), :] = jnp.zeros(
        (blocks, groups * span - depth, g), BF
    )
    mask = mask_in[...].astype(F32)
    scale = 1.0 / (g * g * jnp.sum(mask))
    mode_of = lax.broadcasted_iota(jnp.int32, expand.shape, 0)
    row_lane = lax.broadcasted_iota(jnp.int32, expand.shape, 1)
    expand[...] = jnp.where(mode_of == row_lane // BLK, 1.0, 0.0).astype(BF)

    def send_all(src, dst, sem, devices):
        for device in devices:
            pltpu.make_async_remote_copy(
                src_ref=src(device),
                dst_ref=dst,
                send_sem=sem.at[0],
                recv_sem=sem.at[1],
                device_id=device,
                device_id_type=MESH,
            ).start()

    def wait_all(block, sem):
        both = pltpu.make_async_remote_copy(
            src_ref=block,
            dst_ref=block,
            send_sem=sem.at[0],
            recv_sem=sem.at[1],
            device_id={"frame": 0},
            device_id_type=MESH,
        )
        both.wait_recv()
        both.wait_send()

    frame_peers = [{"frame": lax.rem(me + k, n_frame)} for k in range(1, n_frame)]

    def half_of(at):
        return pl.ds(pl.multiple_of(at * CHUNK, CHUNK), CHUNK)

    def gather(it, at):
        send_all(
            lambda device: ag_send.at[it, half_of(at)],
            ag_recv.at[it, me, half_of(at)],
            ag_sem.at[it, at],
            frame_peers,
        )

    def scatter(at):
        send_all(
            lambda device: rs_send.at[device["frame"], half_of(at)],
            rs_recv.at[me, half_of(at)],
            rs_sem.at[at],
            frame_peers,
        )

    row_of = lax.broadcasted_iota(jnp.int32, (BLK, span), 0)
    lane_of = lax.rem(lax.broadcasted_iota(jnp.int32, (BLK, span), 1), BLK)
    diagonal = row_of == lane_of

    def left_rows(pieces):
        for k in range(lane_blocks):
            width = min(groups * span - k * g * BLK, g * BLK)
            values = dot(pieces[k].astype(BF), expand[:, :width])
            for b in range(width // span):
                cut = values[:, b * span : (b + 1) * span]
                cut = jnp.broadcast_to(cut[:, None, :], (pairs, BLK, span))
                cut = jnp.where(diagonal[None], cut, 0.0)
                first = k * g * BLK + b * span
                rows_left[:, first : first + span] = cut.reshape(pairs * BLK, span).astype(BF)

    def basis_products(out_ref, start, stop):
        lhs = rows_left[:, :depth]

        def block(at, carry):
            rhs = jnp.concatenate([basis[2 * at, :depth, :], basis[2 * at + 1, :depth, :]], axis=1)
            out = dot(lhs, rhs)
            first = pl.multiple_of(at * 2 * BLK, 2 * BLK)
            out_ref[:, pl.ds(first, BLK), :] = out[:, :g].reshape(pairs, BLK, g)
            out_ref[:, pl.ds(first + BLK, BLK), :] = out[:, g:].reshape(pairs, BLK, g)
            return carry

        lax.fori_loop(start, stop, block, 0, unroll=2)

    def relay(k):
        def block(b, carry):
            taken = staged[pl.ds(k * part, part), pl.ds(pl.multiple_of(b * 2 * BLK, 2 * BLK), 2 * BLK), :]
            taken = taken.astype(F32)
            for h in range(2):
                half = taken[:, h * BLK : (h + 1) * BLK].reshape(part * BLK, g)
                basis[2 * b + h, pl.ds(k * part * BLK, part * BLK), :] = half.astype(BF)
            return carry

        lax.fori_loop(0, blocks // 2, block, 0)

    def spectra(it, at):
        for u in range(0, CHUNK, 2):
            q = at * CHUNK + u
            pieces = [
                ag_recv[it, :, q + v].astype(F32).reshape(g, g).astype(BF) for v in range(2)
            ]
            left = dot(inv_in[:, :g], jnp.concatenate(pieces, axis=1))
            out = dot(swap_blocks(left.astype(BF)), fwd_in[...])
            spectrum[it, q] = out[:g]
            spectrum[it, q + 1] = out[g:]

    inverse = 1.0 / (g * g)

    def scalar_steps(it):
        wait_all(sc_recv.at[it, pl.ds(0, n_frame * n_patch - 1)], sc_sem.at[it])
        total = jnp.sum(sc_recv[it], axis=0)
        first = lax.broadcasted_iota(jnp.int32, total.shape, 1) < g // 2
        object_sq = jnp.sum(jnp.where(first, total, 0.0), keepdims=True)
        coeff_sq = jnp.sum(jnp.where(first, 0.0, total), keepdims=True)
        object_count = patches * rows * g * n_frame * n_patch
        coeff_count = pairs * modes * n_frame * n_patch
        object_rms = jnp.sqrt(object_sq / object_count + EPSILON)
        coeff_rms = jnp.sqrt(coeff_sq / coeff_count + EPSILON)
        return STEP_OBJECT / object_rms, STEP_COEFF / coeff_rms

    def patch_chunk(it, at, carry):
        wait_all(ag_recv.at[it, pl.ds(0, n_frame - 1), half_of(at)], ag_sem.at[it, at])
        spectra(it, at)
        if it == 1:

            @pl.when(at == 0)
            def _():
                object_step, coeff_step = scalar_steps(0)
                steps[0:1, :] = jnp.broadcast_to(object_step, (1, g))
                steps[1:2, :] = jnp.broadcast_to(coeff_step, (1, g))

        fwd, inv = fwd_in[...], inv_in[...]
        tabs = (fwd, inv, fwd * BF(inverse), inv * BF(inverse))
        done = []

        def one(q):
            def emit_term(term):
                rs_send[:, q] = term.reshape(n_frame, rows, g).astype(BF)
                done.append(q)
                if len(done) == CHUNK:
                    scatter(at)

            def emit_slope(slope):
                first = pl.multiple_of(q * frames * BLK, frames * BLK)
                for b in range(blocks):
                    cut = slope[b * BLK : (b + 1) * BLK]
                    cut = jnp.concatenate([cut[:, f * g : (f + 1) * g] for f in range(frames)], axis=0)
                    slopes[pl.ds(first, frames * BLK), b * g : (b + 1) * g] = cut.astype(BF)

            picks = [f * patches + q for f in range(frames)]
            phases = [phase[p] for p in picks]
            spec = spectrum[0, q]
            if it == 1:
                phases = [x - steps[1:2, :] * phase_step[p] for x, p in zip(phases, picks)]
                object_step = jnp.concatenate([steps[0:1, :]] * 2, axis=1)
                spec = spec - object_step * spectrum[1, q]
            return patch_steps(
                phases, mask, spec, [observed[p] for p in picks], scale, tabs, emit_term, emit_slope
            )

        interleave([one(at * CHUNK + u) for u in range(CHUNK)])
        return carry

    def coeff_products(start, stop):
        lhs = slopes[...]

        def group(at, carry):
            first = pl.multiple_of(at * span, span)
            rhs = jnp.concatenate([basis[b, pl.ds(first, span), :] for b in range(blocks)], axis=1)
            out = lax.dot_general(lhs, rhs, (((1,), (1,)), ((), ())), preferred_element_type=F32)
            out = jnp.where(diagonal[None], out.reshape(pairs, BLK, span), 0.0)
            wide[at] = jnp.sum(out, axis=1)
            return carry

        lax.fori_loop(start, stop, group, 0, unroll=2)

    def coeff_gradient():
        per = g * BLK // span
        rest = jnp.concatenate(
            [
                jnp.concatenate([wide[k * per + b] for b in range(per)], axis=1)
                for k in range(lane_blocks)
            ],
            axis=0,
        )
        total = 0.0
        for _ in range(3):
            low = rest.astype(BF)
            total = total + lax.dot_general(
                low, expand[...], (((1,), (1,)), ((), ())), preferred_element_type=F32
            )
            rest = rest - low.astype(F32)
        pieces = []
        for k in range(lane_blocks):
            turned[k] = total[k * pairs : (k + 1) * pairs]
            pieces.append(
                jnp.concatenate(
                    [turned[k, pl.ds(f, patches, stride=frames), :] for f in range(frames)], axis=0
                )
            )
        return pieces

    def sum_half(it, at):
        wait_all(rs_recv.at[pl.ds(0, n_frame - 1), half_of(at)], rs_sem.at[at])
        own = rs_send[me, half_of(at)].astype(F32)
        for k in range(1, n_frame):
            own = own + rs_recv[lax.rem(me + k, n_frame), half_of(at)].astype(F32)
        own_grad[half_of(at)] = own
        if it == 0:
            ag_send[1, half_of(at)] = own.astype(BF)
            ag_recv[1, me, half_of(at)] = own.astype(BF)

    def gradients(it):
        sum_half(it, 0)
        coeff_products(0, 2)
        if it == 0:
            gather(1, 0)
        coeff_products(2, groups)
        pieces = coeff_gradient()
        sum_half(it, 1)
        own = own_grad[...]
        object_row = jnp.sum(jnp.sum(own * own, axis=0), axis=0, keepdims=True)
        coeff_row = jnp.sum(sum(piece * piece for piece in pieces), axis=0, keepdims=True)
        first = lax.broadcasted_iota(jnp.int32, (1, g), 1) < g // 2
        object_row = object_row + pltpu.roll(object_row, g // 2, 1)
        coeff_row = coeff_row + pltpu.roll(coeff_row, g // 2, 1)
        row = jnp.where(first, object_row, coeff_row)
        sc_send[it] = row
        slot = me * n_patch + my_patch
        sc_recv[it, slot] = row
        for k in range(lane_blocks):
            kept[k] = pieces[k]
        send_all(lambda device: sc_send.at[it], sc_recv.at[it, slot], sc_sem.at[it], others)
        return pieces

    left_rows([coeff_now[:, k * g : (k + 1) * g] for k in range(lane_blocks)])
    ag_recv[0, me] = ag_send[0]
    pl.semaphore_wait(barrier, len(others))
    gather(0, 0)
    gather(0, 1)
    for k in range(PARTS):
        loads[k].wait()
        relay(k)
    basis_products(phase, 0, blocks // 2)
    load_observed.wait()
    lax.fori_loop(0, patches // CHUNK, functools.partial(patch_chunk, 0), 0)
    pieces = gradients(0)

    gather(1, 1)
    left_rows(pieces)
    object_out[...] = own_grad[...]
    for k in range(lane_blocks):
        old[k] = kept[k]
    basis_products(phase_step, 0, blocks // 2)
    lax.fori_loop(0, patches // CHUNK, functools.partial(patch_chunk, 1), 0)
    gradients(1)
    object_now = object_in[...] - steps[0:1, :][None] * object_out[...]
    object_step, coeff_step = scalar_steps(1)
    object_out[...] = object_now - object_step[None] * own_grad[...]
    for k in range(lane_blocks):
        width = min(g, modes - k * g)
        cut = slice(k * g, k * g + width)
        now = coeff_now[:, k * g : (k + 1) * g] - steps[1:2, :] * old[k]
        coeff_out[:, cut] = (now - coeff_step * kept[k])[:, :width]


def pass_on(coeff_in, object_in, coeff_out, object_out):
    coeff_out[...] = coeff_in[...]
    object_out[...] = object_in[...]


def local(n_frame, n_patch, coeffs, observed, object_field, mode_basis, pupil_mask):
    frames, patches, modes = coeffs.shape
    rows, g = object_field.shape[1:]
    pairs = frames * patches
    blocks = g // BLK
    span = 2 * g
    padded = -(-modes * BLK // span) * span
    lane_blocks = -(-modes // g)
    fwd, inv = tables(g)
    vmem = pl.BlockSpec(memory_space=pltpu.VMEM)
    hbm = pl.BlockSpec(memory_space=pl.ANY)
    dma = pltpu.SemaphoreType.DMA
    sizes = (frames, patches, modes, n_frame, n_patch, rows)
    new_coeffs, new_object = pl.pallas_call(
        functools.partial(kernel, sizes),
        out_shape=[
            jax.ShapeDtypeStruct((pairs, modes), F32),
            jax.ShapeDtypeStruct(object_field.shape, F32),
        ],
        in_specs=[vmem] * 5 + [hbm] * 2,
        out_specs=[vmem, vmem],
        scratch_shapes=[
            pltpu.VMEM((modes, g, g), BF),
            pltpu.VMEM((blocks, padded, g), BF),
            pltpu.VMEM((pairs, g, g), BF),
            pltpu.VMEM((pairs * BLK, padded), BF),
            pltpu.VMEM((pairs, g, g), F32),
            pltpu.VMEM((pairs, g, g), F32),
            pltpu.VMEM((2, patches, g, span), F32),
            pltpu.VMEM((pairs * BLK, blocks * g), BF),
            pltpu.VMEM((lane_blocks * g * BLK // span, pairs, span), F32),
            pltpu.VMEM((pairs, lane_blocks * g), F32),
            pltpu.VMEM((lane_blocks, pairs, g), F32),
            pltpu.VMEM((lane_blocks, pairs, g), F32),
            pltpu.VMEM((lane_blocks, pairs, g), F32),
            pltpu.VMEM((patches, rows, g), F32),
            pltpu.VMEM((g, g * BLK), BF),
            pltpu.VMEM((2, patches, rows, g), BF),
            pltpu.VMEM((2, n_frame, patches, rows, g), BF),
            pltpu.VMEM((n_frame, patches, rows, g), BF),
            pltpu.VMEM((n_frame, patches, rows, g), BF),
            pltpu.VMEM((2, 1, g), F32),
            pltpu.VMEM((2, n_frame * n_patch, 1, g), F32),
            pltpu.VMEM((8, g), F32),
            dma((PARTS,)),
            dma(()),
            dma((2, 2, 2)),
            dma((2, 2)),
            dma((2, 2)),
        ],
        compiler_params=pltpu.CompilerParams(
            collective_id=0, has_side_effects=True, vmem_limit_bytes=62 * 1024 * 1024
        ),
    )(
        coeffs.reshape(pairs, modes),
        object_field,
        pupil_mask,
        fwd,
        inv,
        observed.reshape(pairs, g, g),
        mode_basis,
    )
    new_coeffs, new_object = pl.pallas_call(
        pass_on,
        out_shape=[
            jax.ShapeDtypeStruct(new_coeffs.shape, F32),
            jax.ShapeDtypeStruct(new_object.shape, F32),
        ],
    )(new_coeffs, new_object)
    return new_coeffs.reshape(coeffs.shape), new_object


def solution(mesh):
    in_specs = (
        P("frame", "patch", None),
        P("frame", "patch", None, None),
        P("patch", "frame", None),
        P(),
        P(),
    )
    out_specs = (P("frame", "patch", None), P("patch", "frame", None))
    run = functools.partial(local, mesh.shape["frame"], mesh.shape["patch"])
    return jax.shard_map(run, mesh=mesh, in_specs=in_specs, out_specs=out_specs, check_vma=False)
```

time: 73.5 us -> 65.3 us (0.89)
  Pallas kernels: 69.7 us -> 64.4 us
  local copies, waits for them, and re-layouts: 2.89 us -> 0 us
    pallas_call x1, Pallas kernels: 69.7 us -> 62.9 us  [local(): pl.pallas_call(functools.partial(kernel, sizes), out_shape=[jax.ShapeDtyp...]
    unnamed x2 -> x0, local copies, waits for them, and re-layouts: 2.89 us -> none
    pallas_call x0 -> x1, Pallas kernels: none -> 1.52 us  [local(): pl.pallas_call(pass_on, out_shape=[jax.ShapeDtypeStruct(new_coeffs.shape,...]
where the time goes in v3:
time: 65.3 us; the launch traced here: 65.1 us
  Pallas kernels  64.4 us (99%)
    pallas_call x1, Pallas kernels, local(): pl.pallas_call(functools.partial(kernel, sizes), out_shape=[jax.ShapeDtyp...  62.9 us
    pallas_call x1, Pallas kernels, local(): pl.pallas_call(pass_on, out_shape=[jax.ShapeDtypeStruct(new_coeffs.shape,...  1.52 us

profile of v3, /device:TPU:1, one launch (start us, length us, event | category | flops | bytes accessed | tf_op | source)
XLA Modules:
  0.0 65.1 jit_solution(18150834562140966340)
XLA Ops:
  0.6 62.9 %shard_map.86 = (f32[32,300]{1,0:T(8,128)}, f32[16,8,128]{2,1,0:T(8,128)}) custom-call(f32[32,300]{1,0:T(8,128)} %bitcast.4, f32[16,8,128]{2,1,0:T(8,128)} %object_in.1, s32[128,128]{1,0:T(8,128)} %mask_in.1, bf16[256,256]{1,0:T(8,128)(2,1)} %constant.9.fwd_in, bf16[256,256]{1,0:T(8,128)(2,1)} %constant.10.inv_in, bf16[32,128,128]{2,1,0:T(8,128)(2,1)} %bitcast.3, ...), custom_call_target="tpu_custom_call" | custom-call | tf_op jit(solution)/shard_map/pallas_call | solution.py:500
  63.6 1.5 %shard_map.87 = (f32[32,300]{1,0:T(8,128)}, f32[16,8,128]{2,1,0:T(8,128)}) custom-call(f32[32,300]{1,0:T(8,128)} %get-tuple-element.6.coeff_in, f32[16,8,128]{2,1,0:T(8,128)} %get-tuple-element.7.object_in), custom_call_target="tpu_custom_call" | custom-call | tf_op jit(solution)/shard_map/pallas_call | solution.py:549

commit v4 on v3

--- a/solution.py
+++ b/solution.py
@@ -14,7 +14,6 @@
 STEP_COEFF = 0.2
 CHUNK = 8
 BLK = 8
-PARTS = 10
 LANES = 128
 MESH = pl.DeviceIdType.MESH
 BF = jnp.bfloat16
@@ -79,7 +78,7 @@
     return jnp.asarray(fwd, F32).astype(BF), jnp.asarray(inv, F32).astype(BF)
 
 
-def patch_steps(phases, mask, spec, observed, scale, tabs, emit_term, emit_slope):
+def patch_steps(phases, mask, spec_of, observed, scale, tabs, emit_term, emit_slope):
     t1, t2, t1s, t2s = tabs
     g = LANES
     trig = [sincos(p) for p in phases]
@@ -97,6 +96,7 @@
     otf = dot(t2, swap_blocks(y.astype(BF)))
     yield
     otr, oti = otf[:g], otf[g:]
+    spec = spec_of()
     sr = jnp.concatenate([spec[:, :g]] * 2, axis=1)
     si = jnp.concatenate([spec[:, g:]] * 2, axis=1)
     mr = (sr * otr - si * oti).astype(BF)
@@ -138,6 +138,26 @@
         running += waiting[:1]
         waiting = waiting[1:]
         running = [w for w in running if next(w, "done") is None]
+
+
+def far_first(n_frame, n_patch):
+    def hops(shift):
+        dz, dx, dc, dh, dy = shift
+        across = 2 if dh > dx else (1 if dh or dx else 0)
+        return min(dz, n_frame // 4 - dz) + min(dy, n_patch // 2 - dy) + across
+
+    shifts = [
+        (dz, dx, dc, dh, dy)
+        for dz in range(n_frame // 4)
+        for dx in range(2)
+        for dc in range(2)
+        for dh in range(2)
+        for dy in range(n_patch // 2)
+    ][1:]
+    shifts.sort(key=lambda shift: -hops(shift))
+    frame = [shift for shift in shifts if not (shift[3] or shift[4])]
+    patch = [shift for shift in shifts if not (shift[0] or shift[1] or shift[2])]
+    return frame, patch, shifts
 
 
 def kernel(
@@ -178,6 +198,7 @@
     ag_sem,
     rs_sem,
     sc_sem,
+    joined,
 ):
     frames, patches, modes, n_frame, n_patch, rows = sizes
     g = LANES
@@ -187,30 +208,43 @@
     span = 2 * g
     groups = -(-depth // span)
     lane_blocks = -(-modes // g)
-    part = modes // PARTS
     me = lax.axis_index("frame")
     my_patch = lax.axis_index("patch")
+    frame_shifts, patch_shifts, all_shifts = far_first(n_frame, n_patch)
+
+    def device_at(shift):
+        dz, dx, dc, dh, dy = shift
+        device = {}
+        if dz or dx or dc:
+            z, rest = lax.div(me, 4), lax.rem(me, 4)
+            device["frame"] = (
+                lax.rem(z + dz, n_frame // 4) * 4
+                + lax.rem(lax.div(rest, 2) + dx, 2) * 2
+                + lax.rem(rest + dc, 2)
+            )
+        if dh or dy:
+            half, y = lax.div(my_patch, n_patch // 2), lax.rem(my_patch, n_patch // 2)
+            device["patch"] = lax.rem(half + dh, 2) * (n_patch // 2) + lax.rem(y + dy, n_patch // 2)
+        return device
+
+    frame_peers = [device_at(shift) for shift in frame_shifts]
+    patch_peers = [device_at(shift) for shift in patch_shifts]
+    others = [device_at(shift) for shift in all_shifts]
+
+    barrier = pltpu.get_barrier_semaphore()
+    for device in patch_peers + frame_peers:
+        pl.semaphore_signal(barrier, inc=1, device_id=device, device_id_type=MESH)
 
     loads = [
         pltpu.make_async_copy(
-            basis_hbm.at[pl.ds(k * part, part)], staged.at[pl.ds(k * part, part)], basis_sem.at[k]
+            basis_hbm.at[:, pl.ds(k * 2 * BLK, 2 * BLK), :], staged.at[k], basis_sem.at[k]
         )
-        for k in range(PARTS)
+        for k in range(blocks // 2)
     ]
     for load in loads:
         load.start()
     load_observed = pltpu.make_async_copy(observed_hbm, observed, load_sem)
     load_observed.start()
-
-    others = [
-        {"frame": lax.rem(me + k, n_frame), "patch": lax.rem(my_patch + m, n_patch)}
-        for k in range(n_frame)
-        for m in range(n_patch)
-        if k or m
-    ]
-    barrier = pltpu.get_barrier_semaphore()
-    for device in others:
-        pl.semaphore_signal(barrier, inc=1, device_id=device, device_id_type=MESH)
 
     ag_send[0] = object_in[...].astype(BF)
     coeff_now[...] = jnp.zeros(coeff_now.shape, F32)
@@ -248,8 +282,6 @@
         both.wait_recv()
         both.wait_send()
 
-    frame_peers = [{"frame": lax.rem(me + k, n_frame)} for k in range(1, n_frame)]
-
     def half_of(at):
         return pl.ds(pl.multiple_of(at * CHUNK, CHUNK), CHUNK)
 
@@ -284,40 +316,26 @@
                 first = k * g * BLK + b * span
                 rows_left[:, first : first + span] = cut.reshape(pairs * BLK, span).astype(BF)
 
-    def basis_products(out_ref, start, stop):
+    def basis_product(out_ref, at):
         lhs = rows_left[:, :depth]
-
-        def block(at, carry):
-            rhs = jnp.concatenate([basis[2 * at, :depth, :], basis[2 * at + 1, :depth, :]], axis=1)
-            out = dot(lhs, rhs)
-            first = pl.multiple_of(at * 2 * BLK, 2 * BLK)
-            out_ref[:, pl.ds(first, BLK), :] = out[:, :g].reshape(pairs, BLK, g)
-            out_ref[:, pl.ds(first + BLK, BLK), :] = out[:, g:].reshape(pairs, BLK, g)
-            return carry
-
-        lax.fori_loop(start, stop, block, 0, unroll=2)
+        rhs = jnp.concatenate([basis[2 * at, :depth, :], basis[2 * at + 1, :depth, :]], axis=1)
+        out = dot(lhs, rhs)
+        first = pl.multiple_of(at * 2 * BLK, 2 * BLK)
+        out_ref[:, pl.ds(first, BLK), :] = out[:, :g].reshape(pairs, BLK, g)
+        out_ref[:, pl.ds(first + BLK, BLK), :] = out[:, g:].reshape(pairs, BLK, g)
 
     def relay(k):
-        def block(b, carry):
-            taken = staged[pl.ds(k * part, part), pl.ds(pl.multiple_of(b * 2 * BLK, 2 * BLK), 2 * BLK), :]
-            taken = taken.astype(F32)
-            for h in range(2):
-                half = taken[:, h * BLK : (h + 1) * BLK].reshape(part * BLK, g)
-                basis[2 * b + h, pl.ds(k * part * BLK, part * BLK), :] = half.astype(BF)
-            return carry
-
-        lax.fori_loop(0, blocks // 2, block, 0)
-
-    def spectra(it, at):
-        for u in range(0, CHUNK, 2):
-            q = at * CHUNK + u
-            pieces = [
-                ag_recv[it, :, q + v].astype(F32).reshape(g, g).astype(BF) for v in range(2)
-            ]
-            left = dot(inv_in[:, :g], jnp.concatenate(pieces, axis=1))
-            out = dot(swap_blocks(left.astype(BF)), fwd_in[...])
-            spectrum[it, q] = out[:g]
-            spectrum[it, q + 1] = out[g:]
+        taken = staged[k].astype(F32)
+        for h in range(2):
+            half = taken[:, h * BLK : (h + 1) * BLK].reshape(depth, g)
+            basis[2 * k + h, pl.ds(0, depth), :] = half.astype(BF)
+
+    def spectra(it, q):
+        pieces = [ag_recv[it, :, q + v].astype(F32).reshape(g, g).astype(BF) for v in range(2)]
+        left = dot(inv_in[:, :g], jnp.concatenate(pieces, axis=1))
+        out = dot(swap_blocks(left.astype(BF)), fwd_in[...])
+        spectrum[it, q] = out[:g]
+        spectrum[it, q + 1] = out[g:]
 
     inverse = 1.0 / (g * g)
 
@@ -335,7 +353,8 @@
 
     def patch_chunk(it, at, carry):
         wait_all(ag_recv.at[it, pl.ds(0, n_frame - 1), half_of(at)], ag_sem.at[it, at])
-        spectra(it, at)
+        for u in range(0, CHUNK, 2):
+            spectra(it, at * CHUNK + u)
         if it == 1:
 
             @pl.when(at == 0)
@@ -348,7 +367,16 @@
         tabs = (fwd, inv, fwd * BF(inverse), inv * BF(inverse))
         done = []
 
-        def one(q):
+        def one(u):
+            q = at * CHUNK + u
+
+            def spec_of():
+                spec = spectrum[0, q]
+                if it == 1:
+                    object_step = jnp.concatenate([steps[0:1, :]] * 2, axis=1)
+                    spec = spec - object_step * spectrum[1, q]
+                return spec
+
             def emit_term(term):
                 rs_send[:, q] = term.reshape(n_frame, rows, g).astype(BF)
                 done.append(q)
@@ -364,16 +392,20 @@
 
             picks = [f * patches + q for f in range(frames)]
             phases = [phase[p] for p in picks]
-            spec = spectrum[0, q]
             if it == 1:
                 phases = [x - steps[1:2, :] * phase_step[p] for x, p in zip(phases, picks)]
-                object_step = jnp.concatenate([steps[0:1, :]] * 2, axis=1)
-                spec = spec - object_step * spectrum[1, q]
             return patch_steps(
-                phases, mask, spec, [observed[p] for p in picks], scale, tabs, emit_term, emit_slope
+                phases,
+                mask,
+                spec_of,
+                [observed[p] for p in picks],
+                scale,
+                tabs,
+                emit_term,
+                emit_slope,
             )
 
-        interleave([one(at * CHUNK + u) for u in range(CHUNK)])
+        interleave([one(u) for u in range(CHUNK)])
         return carry
 
     def coeff_products(start, stop):
@@ -387,7 +419,7 @@
             wide[at] = jnp.sum(out, axis=1)
             return carry
 
-        lax.fori_loop(start, stop, group, 0, unroll=2)
+        lax.fori_loop(start, stop, group, 0, unroll=min(4, stop - start))
 
     def coeff_gradient():
         per = g * BLK // span
@@ -445,18 +477,25 @@
         sc_recv[it, slot] = row
         for k in range(lane_blocks):
             kept[k] = pieces[k]
+        if it == 0:
+            pl.semaphore_wait(joined, len(patch_peers))
         send_all(lambda device: sc_send.at[it], sc_recv.at[it, slot], sc_sem.at[it], others)
         return pieces
 
     left_rows([coeff_now[:, k * g : (k + 1) * g] for k in range(lane_blocks)])
     ag_recv[0, me] = ag_send[0]
-    pl.semaphore_wait(barrier, len(others))
-    gather(0, 0)
-    gather(0, 1)
-    for k in range(PARTS):
+    for k in range(blocks // 2):
         loads[k].wait()
         relay(k)
-    basis_products(phase, 0, blocks // 2)
+        if k >= 1:
+            basis_product(phase, k - 1)
+        if k == 1:
+            pl.semaphore_wait(barrier, len(patch_peers + frame_peers))
+            gather(0, 0)
+            gather(0, 1)
+            for device in patch_peers:
+                pl.semaphore_signal(joined, inc=1, device_id=device, device_id_type=MESH)
+    basis_product(phase, blocks // 2 - 1)
     load_observed.wait()
     lax.fori_loop(0, patches // CHUNK, functools.partial(patch_chunk, 0), 0)
     pieces = gradients(0)
@@ -466,7 +505,12 @@
     object_out[...] = own_grad[...]
     for k in range(lane_blocks):
         old[k] = kept[k]
-    basis_products(phase_step, 0, blocks // 2)
+
+    def step_product(at, carry):
+        basis_product(phase_step, at)
+        return carry
+
+    lax.fori_loop(0, blocks // 2, step_product, 0, unroll=4)
     lax.fori_loop(0, patches // CHUNK, functools.partial(patch_chunk, 1), 0)
     gradients(1)
     object_now = object_in[...] - steps[0:1, :][None] * object_out[...]
@@ -506,7 +550,7 @@
         in_specs=[vmem] * 5 + [hbm] * 2,
         out_specs=[vmem, vmem],
         scratch_shapes=[
-            pltpu.VMEM((modes, g, g), BF),
+            pltpu.VMEM((blocks // 2, modes, 2 * BLK, g), BF),
             pltpu.VMEM((blocks, padded, g), BF),
             pltpu.VMEM((pairs, g, g), BF),
             pltpu.VMEM((pairs * BLK, padded), BF),
@@ -528,11 +572,12 @@
             pltpu.VMEM((2, 1, g), F32),
             pltpu.VMEM((2, n_frame * n_patch, 1, g), F32),
             pltpu.VMEM((8, g), F32),
-            dma((PARTS,)),
+            dma((blocks // 2,)),
             dma(()),
             dma((2, 2, 2)),
             dma((2, 2)),
             dma((2, 2)),
+            pltpu.SemaphoreType.REGULAR,
         ],
         compiler_params=pltpu.CompilerParams(
             collective_id=0, has_side_effects=True, vmem_limit_bytes=62 * 1024 * 1024

time: 65.3 us -> 63 us (0.965)
  Pallas kernels: 64.4 us -> 62.2 us
    pallas_call x1, Pallas kernels: 62.9 us -> 60.7 us  [local(): pl.pallas_call(functools.partial(kernel, sizes), out_shape=[jax.ShapeDtyp...]
where the time goes in v4:
time: 63 us; the launch traced here: 62.8 us
  Pallas kernels  62.2 us (99%)
  between operations  0.64 us (1%)
    pallas_call x1, Pallas kernels, local(): pl.pallas_call(functools.partial(kernel, sizes), out_shape=[jax.ShapeDtyp...  60.7 us
    pallas_call x1, Pallas kernels, local(): pl.pallas_call(pass_on, out_shape=[jax.ShapeDtypeStruct(new_coeffs.shape,...  1.52 us

profile of v4, /device:TPU:1, one launch (start us, length us, event | category | flops | bytes accessed | tf_op | source)
XLA Modules:
  0.0 62.8 jit_solution(14205762560775247389)
XLA Ops:
  0.6 60.7 %shard_map.86 = (f32[32,300]{1,0:T(8,128)}, f32[16,8,128]{2,1,0:T(8,128)}) custom-call(f32[32,300]{1,0:T(8,128)} %bitcast.4, f32[16,8,128]{2,1,0:T(8,128)} %object_in.1, s32[128,128]{1,0:T(8,128)} %mask_in.1, bf16[256,256]{1,0:T(8,128)(2,1)} %constant.9.fwd_in, bf16[256,256]{1,0:T(8,128)(2,1)} %constant.10.inv_in, bf16[32,128,128]{2,1,0:T(8,128)(2,1)} %bitcast.3, ...), custom_call_target="tpu_custom_call" | custom-call | tf_op jit(solution)/shard_map/pallas_call | solution.py:544
  61.3 1.5 %shard_map.87 = (f32[32,300]{1,0:T(8,128)}, f32[16,8,128]{2,1,0:T(8,128)}) custom-call(f32[32,300]{1,0:T(8,128)} %get-tuple-element.6.coeff_in, f32[16,8,128]{2,1,0:T(8,128)} %get-tuple-element.7.object_in), custom_call_target="tpu_custom_call" | custom-call | tf_op jit(solution)/shard_map/pallas_call | solution.py:594

commit v5 on v4

--- a/solution.py
+++ b/solution.py
@@ -212,19 +212,27 @@
     my_patch = lax.axis_index("patch")
     frame_shifts, patch_shifts, all_shifts = far_first(n_frame, n_patch)
 
+    z, rest = lax.div(me, 4), lax.rem(me, 4)
+    half, y = lax.div(my_patch, n_patch // 2), lax.rem(my_patch, n_patch // 2)
+    x, core = lax.div(rest, 2), lax.rem(rest, 2)
+    z_at = [z * 4] + [lax.rem(z + d, n_frame // 4) * 4 for d in range(1, n_frame // 4)]
+    x_at, core_at = [x * 2, 2 - x * 2], [core, 1 - core]
+    half_at = [half * (n_patch // 2), (1 - half) * (n_patch // 2)]
+    y_at = [y] + [lax.rem(y + d, n_patch // 2) for d in range(1, n_patch // 2)]
+    frame_at = {
+        (dz, dx, dc): z_at[dz] + x_at[dx] + core_at[dc]
+        for dz in range(n_frame // 4)
+        for dx in range(2)
+        for dc in range(2)
+    }
+    patch_at = {(dh, dy): half_at[dh] + y_at[dy] for dh in range(2) for dy in range(n_patch // 2)}
+
     def device_at(shift):
-        dz, dx, dc, dh, dy = shift
         device = {}
-        if dz or dx or dc:
-            z, rest = lax.div(me, 4), lax.rem(me, 4)
-            device["frame"] = (
-                lax.rem(z + dz, n_frame // 4) * 4
-                + lax.rem(lax.div(rest, 2) + dx, 2) * 2
-                + lax.rem(rest + dc, 2)
-            )
-        if dh or dy:
-            half, y = lax.div(my_patch, n_patch // 2), lax.rem(my_patch, n_patch // 2)
-            device["patch"] = lax.rem(half + dh, 2) * (n_patch // 2) + lax.rem(y + dy, n_patch // 2)
+        if any(shift[:3]):
+            device["frame"] = frame_at[shift[:3]]
+        if any(shift[3:]):
+            device["patch"] = patch_at[shift[3:]]
         return device
 
     frame_peers = [device_at(shift) for shift in frame_shifts]
@@ -419,7 +427,7 @@
             wide[at] = jnp.sum(out, axis=1)
             return carry
 
-        lax.fori_loop(start, stop, group, 0, unroll=min(4, stop - start))
+        lax.fori_loop(start, stop, group, 0, unroll=min(8, stop - start))
 
     def coeff_gradient():
         per = g * BLK // span
@@ -510,7 +518,7 @@
         basis_product(phase_step, at)
         return carry
 
-    lax.fori_loop(0, blocks // 2, step_product, 0, unroll=4)
+    lax.fori_loop(0, blocks // 2, step_product, 0, unroll=8)
     lax.fori_loop(0, patches // CHUNK, functools.partial(patch_chunk, 1), 0)
     gradients(1)
     object_now = object_in[...] - steps[0:1, :][None] * object_out[...]

time: 63 us -> 62.9 us (level)
  no operation moved by 1% of the time
where the time goes in v5:
time: 62.9 us; the launch traced here: 62.7 us
  Pallas kernels  62.1 us (99%)
  between operations  0.64 us (1%)
    pallas_call x1, Pallas kernels, local(): pl.pallas_call(functools.partial(kernel, sizes), out_shape=[jax.ShapeDtyp...  60.5 us
    pallas_call x1, Pallas kernels, local(): pl.pallas_call(pass_on, out_shape=[jax.ShapeDtypeStruct(new_coeffs.shape,...  1.52 us

profile of v5, /device:TPU:1, one launch (start us, length us, event | category | flops | bytes accessed | tf_op | source)
XLA Modules:
  0.0 62.7 jit_solution(8143370009966538282)
XLA Ops:
  0.6 60.5 %shard_map.86 = (f32[32,300]{1,0:T(8,128)}, f32[16,8,128]{2,1,0:T(8,128)}) custom-call(f32[32,300]{1,0:T(8,128)} %bitcast.4, f32[16,8,128]{2,1,0:T(8,128)} %object_in.1, s32[128,128]{1,0:T(8,128)} %mask_in.1, bf16[256,256]{1,0:T(8,128)(2,1)} %constant.9.fwd_in, bf16[256,256]{1,0:T(8,128)(2,1)} %constant.10.inv_in, bf16[32,128,128]{2,1,0:T(8,128)(2,1)} %bitcast.3, ...), custom_call_target="tpu_custom_call" | custom-call | tf_op jit(solution)/shard_map/pallas_call | solution.py:552
  61.2 1.5 %shard_map.87 = (f32[32,300]{1,0:T(8,128)}, f32[16,8,128]{2,1,0:T(8,128)}) custom-call(f32[32,300]{1,0:T(8,128)} %get-tuple-element.6.coeff_in, f32[16,8,128]{2,1,0:T(8,128)} %get-tuple-element.7.object_in), custom_call_target="tpu_custom_call" | custom-call | tf_op jit(solution)/shard_map/pallas_call | solution.py:602
